TPU v7x, 256 devices: a whole 4x4x8 slice. The times are simulated.
256 devices in a mesh: row: 16 (over z_lo, y, core), col: 16 (over x, z_hi).
Axes of the slice: x: 4, y: 4, z: 8 (z_hi: 4, z_lo: 2; z = z_hi * 2 + z_lo), core: 2. Of those that a mesh axis runs over, the one named last changes fastest.
Arguments:
- density: float32 [16, 16, 7, 2, 128, 128], P('row', 'col'), may hold values from -1 to 2, as said below
- hamiltonian: float32 [16, 16, 7, 2, 128, 128], P('row', 'col'), may hold values from -2 to 4, as said below
- offsets: int32 [7, 3], replicated, may hold values from -1 to 1, as said below
- branch: int32 [3], replicated, may hold values from 0 to 1, as said below
Outputs:
- new_density: float32 [16, 16, 7, 2, 128, 128], P('row', 'col')
- grad_density: float32 [16, 16, 7, 2, 128, 128], P('row', 'col')
- totals: float32 [2], replicated
Inputs may be any that keep to these rules, and one draw needn't show every extreme that they name: 7 distinct offsets; (0, 0, 0) is one of them and with each offset its negative (layer step modulo 2) is another; row and column steps lie in -1 to 1, and nonzero row steps and nonzero column steps both occur. `branch`: each entry is 0 or 1, and not all entries are equal. `density`: the matrix is symmetric: entry [p, q, t, s] is the transpose of the entry of the opposite offset at the transposed block position. `hamiltonian`: the matrix is symmetric, in the same sense as the density.
All inputs are finite; a program needn't handle non-finite values.
Results may differ from a plain program's by a relative error of at most 0.0003.
Values sent between devices are 32-bit elements; how exact they have to be, the bound alone decides.
A program may use at most 128 MiB of HBM per device.

v0:
```python
import functools

import jax
import jax.numpy as jnp
from jax import lax
from jax.sharding import Mesh
from jax.sharding import PartitionSpec as P

ROW = ("row_0", "row_1", "row_2")
COL = ("col_0", "col_1")
ROW_COL = ("row_0", "row_1", "row_2", "col_0", "col_1")


FULL_PRECISION = lax.Precision.HIGHEST


def with_halo(block, sides, width):
    for axis, dim in sides:
        count = lax.axis_size(axis)
        forward = [(i, i + 1) for i in range(count - 1)]
        forward.append((count - 1, 0))
        backward = [(target, source) for source, target in forward]
        low = lax.ppermute(
            lax.slice_in_dim(block, block.shape[dim] - width, None, axis=dim), axis, forward
        )
        high = lax.ppermute(lax.slice_in_dim(block, 0, width, axis=dim), axis, backward)
        block = jnp.concatenate([low, block, high], axis=dim)
    return block


def one_axis_at_a_time(array, axes):
    return functools.reduce(lax.psum, axes, array)


def pair_tables(offsets, row_count, col_count, layer_count):
    moduli = jnp.array([row_count, col_count, layer_count], jnp.int32)
    summed = offsets[:, None, :] + offsets[None, :, :]
    differ = summed[None, :, :, :] - offsets[:, None, None, :]
    matches = jnp.all(differ % moduli == 0, axis=-1).astype(jnp.int32)
    partner = jnp.argmax(matches, axis=2)
    usable = jnp.max(matches, axis=2)
    return (partner, usable)


def sparse_product(left_rim, right_rim, offsets, partner, usable):
    count_offsets = offsets.shape[0]
    layer_count = left_rim.shape[2]
    col_pick = 1 - offsets[:, 1]
    row_pick = 1 + offsets[:, 0]
    layer_pick = (jnp.arange(layer_count, dtype=jnp.int32)[None, :] + offsets[:, 2:3]) % layer_count
    left_slots = jnp.arange(count_offsets, dtype=jnp.int32)

    def one_target(target):
        partners_row = partner[target]
        keep_mask = usable[target].astype(jnp.float32)
        left_part = left_rim[col_pick[partners_row], left_slots] * keep_mask[:, None, None, None]
        right_part = right_rim[row_pick[:, None], partners_row[:, None], layer_pick]
        return jnp.einsum("tsab,tsbc->sac", left_part, right_part, precision=FULL_PRECISION)

    return lax.map(one_target, jnp.arange(count_offsets, dtype=jnp.int32))


def iterate_rims(field):
    rows_rim = with_halo(field, ((ROW, 0),), 1)[:, 0]
    cols_rim = with_halo(field, ((COL, 1),), 1)[0]
    return (cols_rim, rows_rim)


def outer_rims(field):
    rows_rim = with_halo(field, ((ROW, 0),), 1)[:, 0]
    cols_rim = with_halo(field, ((COL, 1),), 1)[0]
    return (cols_rim, rows_rim)


def local(density, hamiltonian, offsets, branch):
    row_count = lax.axis_size(ROW)
    col_count = lax.axis_size(COL)
    step_count = branch.shape[0]
    layer_count = density.shape[3]
    block_size = density.shape[4]
    matrix_order = block_size * layer_count * row_count * col_count
    partner, usable = pair_tables(offsets, row_count, col_count, layer_count)
    zero_slot = jnp.all(offsets == 0, axis=1).astype(jnp.float32)
    identity_part = zero_slot[:, None, None, None] * jnp.eye(block_size, dtype=jnp.float32)
    branch_signs = (2 * branch - 1).astype(jnp.float32)
    density_rows = with_halo(density, ((ROW, 0),), 1)[:, 0]
    density_cols = with_halo(density, ((COL, 1),), 1)[0]
    density_rims = (density_cols, density_rows)
    iterates = [density]
    rims = [density_rims]
    for step in range(step_count):
        current = iterates[-1]
        square = sparse_product(rims[-1][0], rims[-1][1], offsets, partner, usable)[None, None]
        following = current + branch_signs[step] * (current - square)
        iterates.append(following)
        if step + 1 < step_count:
            rims.append(iterate_rims(following))
    new_density = iterates[-1]
    global_sums = (
        one_axis_at_a_time(jnp.sum(hamiltonian * new_density), ROW_COL),
        one_axis_at_a_time(jnp.sum(new_density * identity_part), ROW_COL),
    )
    totals = jnp.stack(global_sums) / matrix_order
    excess = totals[1] - 0.5
    outer_grad = hamiltonian + excess * identity_part
    last = step_count - 1
    last_cols, last_rows = rims[last]
    cotangent_rows = with_halo(outer_grad, ((ROW, 0),), 1)[:, 0]
    cotangent_cols = with_halo(outer_grad, ((COL, 1),), 1)[0]
    cross_terms = sparse_product(
        cotangent_cols, last_rows, offsets, partner, usable
    ) + sparse_product(last_cols, cotangent_rows, offsets, partner, usable)
    cross_terms = cross_terms[None, None]
    outer_grad = (1.0 + branch_signs[last]) * outer_grad - branch_signs[last] * cross_terms
    for step in range(last - 1, -1, -1):
        grad_cols, grad_rows = outer_rims(outer_grad)
        step_cols, step_rows = rims[step]
        cross_terms = sparse_product(
            grad_cols, step_rows, offsets, partner, usable
        ) + sparse_product(step_cols, grad_rows, offsets, partner, usable)
        outer_grad = (1.0 + branch_signs[step]) * outer_grad - branch_signs[step] * cross_terms[
            None, None
        ]
    return (new_density, outer_grad, totals)


def solution(mesh):
    finer = Mesh(mesh.devices.reshape(2, 4, 2, 4, 4), ("row_0", "row_1", "row_2", "col_0", "col_1"))
    return jax.shard_map(
        local,
        mesh=finer,
        in_specs=(
            P(ROW, COL, None, None, None, None),
            P(ROW, COL, None, None, None, None),
            P(),
            P(),
        ),
        out_specs=(P(ROW, COL, None, None, None, None), P(ROW, COL, None, None, None, None), P()),
        check_vma=False,
    )
```

profile of v0, /device:TPU:32, one launch (start us, length us, event | category | flops | bytes accessed | tf_op | source)
XLA Modules:
  0.0 1012.9 jit_solution(6066435808309570010)
XLA Ops:
  0.7 3.8 collective-permute-start.3
  4.6 3.3 collective-permute-start
  7.8 4.3 collective-permute-start.1
  18.6 22.7 %collective-permute-done.2 = f32[1,1,7,2,128,128]{5,4,3,2,0,1:T(8,128)S(1)} collective-permute-done((f32[1,1,7,2,128,128]{5,4,3,2,0,1:T(8,128)}, f32[1,1,7,2,128,128]{5,4,3,2,0,1:T(8,128)S(1)}, u32[]{:S(2)}, u32[]{:S(2)}) %collective-permute-start.2) | collective-permute-done | bytes 917536 | tf_op jit(solution)/shard_map/ppermute | solution.py:23
  41.9 3.4 maximum_bitcast_fusion.1
  45.3 13.5 %collective-permute-done.1 = f32[1,1,7,2,128,128]{5,4,3,2,1,0:T(8,128)} collective-permute-done((f32[1,1,7,2,128,128]{5,4,3,2,1,0:T(8,128)}, f32[1,1,7,2,128,128]{5,4,3,2,1,0:T(8,128)}, u32[]{:S(2)}, u32[]{:S(2)}) %collective-permute-start.1) | collective-permute-done | bytes 917536 | tf_op jit(solution)/shard_map/ppermute | solution.py:26
  58.8 3.2 maximum_bitcast_fusion
  63.0 70.1 %while.117 = (s32[]{:T(128)}, f32[7,2,128,128]{3,2,1,0:T(8,128)}, s32[7]{0:T(128)S(1)}, s32[7,7]{1,0:T(8,128)S(1)}, s32[7]{0:T(128)S(1)}, /*index=5*/f32[3,7,2,1...) while((s32[]{:T(128)}, f32[7,2,128,128]{3,2,1,0:T(8,128)}, ...), condition=%wide.region_4.5_spmd.clone.clone, body=%wide.region_3.4_spmd.clone.clone.sunk | while | flops 352552384 | bytes 5641867 | solution.py:60
  68.8 2.4 gather_fusion
  78.9 2.4 gather_fusion
  88.9 2.4 gather_fusion
  98.9 2.4 gather_fusion
  108.9 2.4 gather_fusion
  118.9 2.4 gather_fusion
  128.9 2.4 gather_fusion
  135.2 3.8 collective-permute-start.7
  139.0 3.6 collective-permute-start.4
  142.6 2.7 collective-permute-start.5
  145.3 33.4 %collective-permute-done.6 = f32[1,1,7,2,128,128]{5,4,3,2,1,0:T(8,128)S(1)} collective-permute-done((f32[1,1,7,2,128,128]{5,4,3,2,1,0:T(8,128)S(1)}, f32[1,1,7,2,128,128]{5,4,3,2,1,0:T(8,128)S(1)}, u32[]{:S(2)}, u32[]{:S(2)}) %collective-permute-start.6) | collective-permute-done | bytes 917536 | tf_op jit(solution)/shard_map/ppermute | solution.py:23
  178.7 3.1 maximum_bitcast_fusion.3
  181.8 9.8 collective-permute-done.5
  191.6 3.2 maximum_bitcast_fusion.2
  194.8 65.7 %while.118 = (s32[]{:T(128)}, f32[7,2,128,128]{3,2,1,0:T(8,128)S(1)}, s32[7]{0:T(128)S(1)}, s32[7,7]{1,0:T(8,128)S(1)}, s32[7]{0:T(128)S(1)}, /*index=5*/f32[3,7...) while((s32[]{:T(128)}, ...), condition=%wide.region_6.7_spmd.clone.clone, body=%wide.region_5.6_spmd.clone.clone.sunk | while | flops 352552384 | bytes 5641843 | solution.py:60
  200.7 2.4 gather_fusion.3
  210.1 2.4 gather_fusion.3
  219.5 2.4 gather_fusion.3
  228.9 2.4 gather_fusion.3
  264.2 3.8 collective-permute-start.11
  269.4 4.9 collective-permute-start.9
  274.5 30.5 %collective-permute-done.10 = f32[1,1,7,2,128,128]{5,4,3,2,1,0:T(8,128)S(1)} collective-permute-done((f32[1,1,7,2,128,128]{5,4,3,2,1,0:T(8,128)S(1)}, f32[1,1,7,2,128,128]{5,4,3,2,1,0:T(8,128)S(1)}, u32[]{:S(2)}, u32[]{:S(2)}) %collective-permute-start.10) | collective-permute-done | bytes 917536 | tf_op jit(solution)/shard_map/ppermute | solution.py:23
  307.3 3.2 maximum_bitcast_fusion.5
  310.5 8.1 collective-permute-done.9
  318.6 3.0 maximum_bitcast_fusion.4
  322.7 70.1 %while.119 = (s32[]{:T(128)}, f32[7,2,128,128]{3,2,1,0:T(8,128)}, s32[7]{0:T(128)S(1)}, s32[7,7]{1,0:T(8,128)S(1)}, s32[7]{0:T(128)S(1)}, /*index=5*/f32[3,7,2,1...) while((s32[]{:T(128)}, f32[7,2,128,128]{3,2,1,0:T(8,128)}, ...), condition=%wide.region_8.9_spmd.clone.clone, body=%wide.region_7.8_spmd.clone.clone.sunk | while | flops 352552384 | bytes 5641867 | solution.py:60
  392.8 4.0 multiply_reduce_fusion.1
  396.8 5.8 all-reduce.4
  402.6 8.3 all-reduce.2
  411.0 3.1 all-reduce.3
  414.1 10.7 %all-reduce.1 = (f32[]{:T(128)}, f32[]{:T(128)}) all-reduce(f32[]{:T(128)} %get-tuple-element.1354, f32[]{:T(128)} %get-tuple-element.1355), channel_id=1, replica_groups=mesh['row_0'=2,'row_1'=4,'row_2'=2,'col_0'=4,'col_1'=4] {'col_0'}, use_global_device_ids=true, to_apply=%region_20.21 | all-reduce | flops 2 | bytes 16 | tf_op jit(solution)/shard_map/psum | solution.py:32
  424.8 12.6 %all-reduce = (f32[1]{0:T(128)}, f32[1]{0:T(128)}) all-reduce(f32[1]{0:T(128)} %bitcast.19, f32[1]{0:T(128)} %bitcast.18), channel_id=1, replica_groups=mesh['row_0'=2,'row_1'=4,'row_2'=2,'col_0'=4,'col_1'=4] {'col_1'}, use_global_device_ids=true, to_apply=%region_21.22 | all-reduce | flops 2 | bytes 16 | tf_op jit(solution)/shard_map/psum | solution.py:32
  440.3 3.8 collective-permute-start.15
  444.9 6.4 collective-permute-start.13
  451.2 33.1 %collective-permute-done.14 = f32[1,1,7,2,128,128]{5,4,3,2,1,0:T(8,128)S(1)} collective-permute-done((f32[1,1,7,2,128,128]{5,4,3,2,1,0:T(8,128)S(1)}, f32[1,1,7,2,128,128]{5,4,3,2,1,0:T(8,128)S(1)}, u32[]{:S(2)}, u32[]{:S(2)}) %collective-permute-start.14) | collective-permute-done | bytes 917536 | tf_op jit(solution)/shard_map/ppermute | solution.py:23
  487.1 67.8 %while.121 = (s32[]{:T(128)}, f32[7,2,128,128]{3,2,1,0:T(8,128)}, s32[7]{0:T(128)S(1)}, s32[7,7]{1,0:T(8,128)S(1)}, s32[7]{0:T(128)S(1)}, /*index=5*/f32[3,7,2,1...) while((s32[]{:T(128)}, f32[7,2,128,128]{3,2,1,0:T(8,128)}, ...), condition=%wide.region_25.26_spmd.clone.clone, body=%wide.region_24.25_spmd.clone.clone.sunk | while | flops 352552384 | bytes 5641867 | solution.py:60
  554.9 3.4 maximum_bitcast_fusion.6
  558.4 65.9 %while.120 = (s32[]{:T(128)}, f32[7,2,128,128]{3,2,1,0:T(8,128)S(1)}, s32[7]{0:T(128)S(1)}, s32[7,7]{1,0:T(8,128)S(1)}, s32[7]{0:T(128)S(1)}, /*index=5*/f32[3,7...) while((s32[]{:T(128)}, ...), condition=%wide.region_23.24_spmd.clone.clone, body=%wide.region_22.23_spmd.clone.clone.sunk | while | flops 352552384 | bytes 5641843 | solution.py:60
  625.2 2.6 bitcast_subtract_fusion.2
  628.0 3.8 collective-permute-start.19
  632.5 6.2 collective-permute-start.17
  638.7 33.5 %collective-permute-done.18 = f32[1,1,7,2,128,128]{5,4,3,2,1,0:T(8,128)S(1)} collective-permute-done((f32[1,1,7,2,128,128]{5,4,3,2,1,0:T(8,128)S(1)}, f32[1,1,7,2,128,128]{5,4,3,2,1,0:T(8,128)S(1)}, u32[]{:S(2)}, u32[]{:S(2)}) %collective-permute-start.18) | collective-permute-done | bytes 917536 | tf_op jit(solution)/shard_map/ppermute | solution.py:23
  675.1 71.5 %while.123 = (s32[]{:T(128)}, f32[7,2,128,128]{3,2,1,0:T(8,128)}, s32[7]{0:T(128)S(1)}, s32[7,7]{1,0:T(8,128)S(1)}, s32[7]{0:T(128)S(1)}, /*index=5*/f32[3,7,2,1...) while((s32[]{:T(128)}, f32[7,2,128,128]{3,2,1,0:T(8,128)}, ...), condition=%wide.region_29.30_spmd.clone.clone, body=%wide.region_28.29_spmd.clone.clone.sunk | while | flops 352552384 | bytes 5641867 | solution.py:60
  746.6 3.5 maximum_bitcast_fusion.8
  751.1 71.5 %while.122 = (s32[]{:T(128)}, f32[7,2,128,128]{3,2,1,0:T(8,128)}, s32[7]{0:T(128)S(1)}, s32[7,7]{1,0:T(8,128)S(1)}, s32[7]{0:T(128)S(1)}, /*index=5*/f32[3,7,2,1...) while((s32[]{:T(128)}, f32[7,2,128,128]{3,2,1,0:T(8,128)}, ...), condition=%wide.region_27.28_spmd.clone.clone, body=%wide.region_26.27_spmd.clone.clone.sunk | while | flops 352552384 | bytes 5641867 | solution.py:60
  818.4 2.4 gather_fusion.15
  822.6 3.3 bitcast_subtract_fusion.1
  825.9 3.9 collective-permute-start.23
  830.6 6.2 collective-permute-start.21
  836.8 32.6 %collective-permute-done.22 = f32[1,1,7,2,128,128]{5,4,3,2,1,0:T(8,128)S(1)} collective-permute-done((f32[1,1,7,2,128,128]{5,4,3,2,1,0:T(8,128)}, f32[1,1,7,2,128,128]{5,4,3,2,1,0:T(8,128)S(1)}, u32[]{:S(2)}, u32[]{:S(2)}) %collective-permute-start.22) | collective-permute-done | bytes 917536 | tf_op jit(solution)/shard_map/ppermute | solution.py:23
  869.4 3.1 maximum_bitcast_fusion.11
  872.6 67.2 %while.125 = (s32[]{:T(128)}, f32[7,2,128,128]{3,2,1,0:T(8,128)S(1)}, s32[7]{0:T(128)S(1)}, s32[7,7]{1,0:T(8,128)S(1)}, s32[7]{0:T(128)S(1)}, /*index=5*/f32[3,7...) while((s32[]{:T(128)}, ...), condition=%wide.region_33.34_spmd.clone.clone, body=%wide.region_32.33_spmd.clone.clone.sunk | while | flops 352552384 | bytes 5641843 | solution.py:60
  939.8 4.0 maximum_bitcast_fusion.10
  943.9 65.6 %while.124 = (s32[]{:T(128)}, f32[7,2,128,128]{3,2,1,0:T(8,128)S(1)}, s32[7]{0:T(128)S(1)}, s32[7,7]{1,0:T(8,128)S(1)}, s32[7]{0:T(128)S(1)}, /*index=5*/f32[3,7...) while((s32[]{:T(128)}, ...), condition=%wide.region_31.32_spmd.clone.clone, body=%wide.region_30.31_spmd.clone.clone.sunk | while | flops 352552384 | bytes 5641843 | solution.py:60
  987.2 2.4 gather_fusion.21
  1009.5 3.2 bitcast_subtract_fusion
  (885 shorter events, 487.3 us)
Async XLA Ops:
  0.6 40.7 %collective-permute-start.2 = (f32[1,1,7,2,128,128]{5,4,3,2,0,1:T(8,128)}, f32[1,1,7,2,128,128]{5,4,3,2,0,1:T(8,128)S(1)}, u32[]{:S(2)}, u32[]{:S(2)}) collective-permute-start(f32[1,1,7,2,128,128]{5,4,3,2,0,1:T(8,128)} %bitcast.631), channel_id=1, source_target_pairs={{0,16},{16,32},{32,48},{48,64},{64,80},{80,96},{96,112},{112,128},... | collective-permute-start | bytes 2752520 | tf_op jit(solution)/shard_map/ppermute | solution.py:23
  0.7 41.2 %collective-permute-start.3 = (f32[1,1,7,2,128,128]{5,4,3,2,0,1:T(8,128)}, f32[1,1,7,2,128,128]{5,4,3,2,0,1:T(8,128)}, u32[]{:S(2)}, u32[]{:S(2)}) collective-permute-start(f32[1,1,7,2,128,128]{5,4,3,2,0,1:T(8,128)} %bitcast.632), channel_id=1, source_target_pairs={{16,0},{32,16},{48,32},{64,48},{80,64},{96,80},{112,96},{128,112},... | collective-permute-start | bytes 2752520 | tf_op jit(solution)/shard_map/ppermute | solution.py:26
  4.6 40.8 %collective-permute-start = (f32[1,1,7,2,128,128]{5,4,3,2,1,0:T(8,128)}, f32[1,1,7,2,128,128]{5,4,3,2,1,0:T(8,128)S(1)}, u32[]{:S(2)}, u32[]{:S(2)}) collective-permute-start(f32[1,1,7,2,128,128]{5,4,3,2,1,0:T(8,128)} %param.23), channel_id=1, source_target_pairs={{0,1},{1,2},{2,3},{3,4},{4,5},{5,6},{6,7},{7,8},{8,9},{9,10},{10,1... | collective-permute-start | bytes 2752520 | tf_op jit(solution)/shard_map/ppermute | solution.py:23
  7.8 51.0 %collective-permute-start.1 = (f32[1,1,7,2,128,128]{5,4,3,2,1,0:T(8,128)}, f32[1,1,7,2,128,128]{5,4,3,2,1,0:T(8,128)}, u32[]{:S(2)}, u32[]{:S(2)}) collective-permute-start(f32[1,1,7,2,128,128]{5,4,3,2,1,0:T(8,128)} %param.23), channel_id=1, source_target_pairs={{1,0},{2,1},{3,2},{4,3},{5,4},{6,5},{7,6},{8,7},{9,8},{10,9},{11,1... | collective-permute-start | bytes 2752520 | tf_op jit(solution)/shard_map/ppermute | solution.py:26
  18.6 40.2 %copy-start.2 = (f32[1,1,7,2,128,128]{5,4,3,2,1,0:T(8,128)S(1)}, f32[1,1,7,2,128,128]{5,4,3,2,1,0:T(8,128)}, u32[]{:S(2)}) copy-start(f32[1,1,7,2,128,128]{5,4,3,2,1,0:T(8,128)} %param.23) | copy-start | bytes 2752516
  135.1 56.5 %copy-start = (f32[1,1,7,2,128,128]{5,4,3,2,1,0:T(8,128)}, f32[1,1,7,2,128,128]{5,4,3,2,1,0:T(8,128)S(1)}, u32[]{:S(2)}) copy-start(f32[1,1,7,2,128,128]{5,4,3,2,1,0:T(8,128)S(1)} %fusion.221) | copy-start | bytes 2752516
  135.1 43.6 %collective-permute-start.6 = (f32[1,1,7,2,128,128]{5,4,3,2,1,0:T(8,128)S(1)}, f32[1,1,7,2,128,128]{5,4,3,2,1,0:T(8,128)S(1)}, u32[]{:S(2)}, u32[]{:S(2)}) collective-permute-start(f32[1,1,7,2,128,128]{5,4,3,2,1,0:T(8,128)S(1)} %fusion.221), channel_id=1, source_target_pairs={{0,16},{16,32},{32,48},{48,64},{64,80},{80,96},{96,112},{112,128},... | collective-permute-start | bytes 2752520 | tf_op jit(solution)/shard_map/ppermute | solution.py:23
  135.2 43.5 %collective-permute-start.7 = (f32[1,1,7,2,128,128]{5,4,3,2,1,0:T(8,128)S(1)}, f32[1,1,7,2,128,128]{5,4,3,2,1,0:T(8,128)}, u32[]{:S(2)}, u32[]{:S(2)}) collective-permute-start(f32[1,1,7,2,128,128]{5,4,3,2,1,0:T(8,128)S(1)} %fusion.221), channel_id=1, source_target_pairs={{16,0},{32,16},{48,32},{64,48},{80,64},{96,80},{112,96},{128,112},... | collective-permute-start | bytes 2752520 | tf_op jit(solution)/shard_map/ppermute | solution.py:26
  139.0 42.7 %collective-permute-start.4 = (f32[1,1,7,2,128,128]{5,4,3,2,1,0:T(8,128)S(1)}, f32[1,1,7,2,128,128]{5,4,3,2,1,0:T(8,128)S(1)}, u32[]{:S(2)}, u32[]{:S(2)}) collective-permute-start(f32[1,1,7,2,128,128]{5,4,3,2,1,0:T(8,128)S(1)} %fusion.221), channel_id=1, source_target_pairs={{0,1},{1,2},{2,3},{3,4},{4,5},{5,6},{6,7},{7,8},{8,9},{9,10},{10,1... | collective-permute-start | bytes 2752520 | tf_op jit(solution)/shard_map/ppermute | solution.py:23
  142.6 49.0 %collective-permute-start.5 = (f32[1,1,7,2,128,128]{5,4,3,2,1,0:T(8,128)S(1)}, f32[1,1,7,2,128,128]{5,4,3,2,1,0:T(8,128)}, u32[]{:S(2)}, u32[]{:S(2)}) collective-permute-start(f32[1,1,7,2,128,128]{5,4,3,2,1,0:T(8,128)S(1)} %fusion.221), channel_id=1, source_target_pairs={{1,0},{2,1},{3,2},{4,3},{5,4},{6,5},{7,6},{8,7},{9,8},{10,9},{11,1... | collective-permute-start | bytes 2752520 | tf_op jit(solution)/shard_map/ppermute | solution.py:26
  260.6 0.9 copy-start.3
  260.6 13.8 %copy-start.6 = (s32[7,3]{0,1:T(4,128)S(1)}, s32[7,3]{0,1:T(4,128)}, u32[]{:S(2)}) copy-start(s32[7,3]{0,1:T(4,128)} %param.25) | copy-start | bytes 256
  263.7 41.3 %collective-permute-start.10 = (f32[1,1,7,2,128,128]{5,4,3,2,1,0:T(8,128)S(1)}, f32[1,1,7,2,128,128]{5,4,3,2,1,0:T(8,128)S(1)}, u32[]{:S(2)}, u32[]{:S(2)}) collective-permute-start(f32[1,1,7,2,128,128]{5,4,3,2,1,0:T(8,128)S(1)} %fusion.219), channel_id=1, source_target_pairs={{0,16},{16,32},{32,48},{48,64},{64,80},{80,96},{96,112},{112,128},... | collective-permute-start | bytes 2752520 | tf_op jit(solution)/shard_map/ppermute | solution.py:23
  264.2 43.1 %collective-permute-start.11 = (f32[1,1,7,2,128,128]{5,4,3,2,1,0:T(8,128)S(1)}, f32[1,1,7,2,128,128]{5,4,3,2,1,0:T(8,128)}, u32[]{:S(2)}, u32[]{:S(2)}) collective-permute-start(f32[1,1,7,2,128,128]{5,4,3,2,1,0:T(8,128)S(1)} %fusion.219), channel_id=1, source_target_pairs={{16,0},{32,16},{48,32},{64,48},{80,64},{96,80},{112,96},{128,112},... | collective-permute-start | bytes 2752520 | tf_op jit(solution)/shard_map/ppermute | solution.py:26
  268.1 42.5 %collective-permute-start.8 = (f32[1,1,7,2,128,128]{5,4,3,2,1,0:T(8,128)S(1)}, f32[1,1,7,2,128,128]{5,4,3,2,1,0:T(8,128)S(1)}, u32[]{:S(2)}, u32[]{:S(2)}) collective-permute-start(f32[1,1,7,2,128,128]{5,4,3,2,1,0:T(8,128)S(1)} %fusion.219), channel_id=1, source_target_pairs={{0,1},{1,2},{2,3},{3,4},{4,5},{5,6},{6,7},{7,8},{8,9},{9,10},{10,1... | collective-permute-start | bytes 2752520 | tf_op jit(solution)/shard_map/ppermute | solution.py:23
  269.4 49.2 %collective-permute-start.9 = (f32[1,1,7,2,128,128]{5,4,3,2,1,0:T(8,128)S(1)}, f32[1,1,7,2,128,128]{5,4,3,2,1,0:T(8,128)}, u32[]{:S(2)}, u32[]{:S(2)}) collective-permute-start(f32[1,1,7,2,128,128]{5,4,3,2,1,0:T(8,128)S(1)} %fusion.219), channel_id=1, source_target_pairs={{1,0},{2,1},{3,2},{4,3},{5,4},{6,5},{7,6},{8,7},{9,8},{10,9},{11,1... | collective-permute-start | bytes 2752520 | tf_op jit(solution)/shard_map/ppermute | solution.py:26
  392.8 47.3 %copy-start.1 = (f32[1,1,7,2,128,128]{5,4,3,2,1,0:T(8,128)S(1)}, f32[1,1,7,2,128,128]{5,4,3,2,1,0:T(8,128)}, u32[]{:S(2)}) copy-start(f32[1,1,7,2,128,128]{5,4,3,2,1,0:T(8,128)} %param.24) | copy-start | bytes 2752516
  438.8 47.4 %copy-start.7 = (f32[2]{0:T(128)}, f32[2]{0:T(128)S(1)}, u32[]{:S(2)}) copy-start(f32[2]{0:T(128)S(1)} %maximum_multiply_fusion) | copy-start | bytes 28
  440.2 44.2 %collective-permute-start.14 = (f32[1,1,7,2,128,128]{5,4,3,2,1,0:T(8,128)S(1)}, f32[1,1,7,2,128,128]{5,4,3,2,1,0:T(8,128)S(1)}, u32[]{:S(2)}, u32[]{:S(2)}) collective-permute-start(f32[1,1,7,2,128,128]{5,4,3,2,1,0:T(8,128)S(1)} %broadcast_add_fusion), channel_id=1, source_target_pairs={{0,16},{16,32},{32,48},{48,64},{64,80},{80,96},{96,112},{112,128},... | collective-permute-start | bytes 2752520 | tf_op jit(solution)/shard_map/ppermute | solution.py:23
  440.3 44.1 %collective-permute-start.15 = (f32[1,1,7,2,128,128]{5,4,3,2,1,0:T(8,128)S(1)}, f32[1,1,7,2,128,128]{5,4,3,2,1,0:T(8,128)S(1)}, u32[]{:S(2)}, u32[]{:S(2)}) collective-permute-start(f32[1,1,7,2,128,128]{5,4,3,2,1,0:T(8,128)S(1)} %broadcast_add_fusion), channel_id=1, source_target_pairs={{16,0},{32,16},{48,32},{64,48},{80,64},{96,80},{112,96},{128,112},... | collective-permute-start | bytes 2752520 | tf_op jit(solution)/shard_map/ppermute | solution.py:26
  444.8 110.1 %collective-permute-start.12 = (f32[1,1,7,2,128,128]{5,4,3,2,1,0:T(8,128)S(1)}, f32[1,1,7,2,128,128]{5,4,3,2,1,0:T(8,128)}, u32[]{:S(2)}, u32[]{:S(2)}) collective-permute-start(f32[1,1,7,2,128,128]{5,4,3,2,1,0:T(8,128)S(1)} %broadcast_add_fusion), channel_id=1, source_target_pairs={{0,1},{1,2},{2,3},{3,4},{4,5},{5,6},{6,7},{7,8},{8,9},{9,10},{10,1... | collective-permute-start | bytes 2752520 | tf_op jit(solution)/shard_map/ppermute | solution.py:23
  444.9 110.0 %collective-permute-start.13 = (f32[1,1,7,2,128,128]{5,4,3,2,1,0:T(8,128)S(1)}, f32[1,1,7,2,128,128]{5,4,3,2,1,0:T(8,128)}, u32[]{:S(2)}, u32[]{:S(2)}) collective-permute-start(f32[1,1,7,2,128,128]{5,4,3,2,1,0:T(8,128)S(1)} %broadcast_add_fusion), channel_id=1, source_target_pairs={{1,0},{2,1},{3,2},{4,3},{5,4},{6,5},{7,6},{8,7},{9,8},{10,9},{11,1... | collective-permute-start | bytes 2752520 | tf_op jit(solution)/shard_map/ppermute | solution.py:26
  624.3 0.9 copy-start.4
  627.9 44.4 %collective-permute-start.18 = (f32[1,1,7,2,128,128]{5,4,3,2,1,0:T(8,128)S(1)}, f32[1,1,7,2,128,128]{5,4,3,2,1,0:T(8,128)S(1)}, u32[]{:S(2)}, u32[]{:S(2)}) collective-permute-start(f32[1,1,7,2,128,128]{5,4,3,2,1,0:T(8,128)S(1)} %bitcast_subtract_fusion.2), channel_id=1, source_target_pairs={{0,16},{16,32},{32,48},{48,64},{64,80},{80,96},{96,112},{112,128},... | collective-permute-start | bytes 2752520 | tf_op jit(solution)/shard_map/ppermute | solution.py:23
  628.0 44.3 %collective-permute-start.19 = (f32[1,1,7,2,128,128]{5,4,3,2,1,0:T(8,128)S(1)}, f32[1,1,7,2,128,128]{5,4,3,2,1,0:T(8,128)S(1)}, u32[]{:S(2)}, u32[]{:S(2)}) collective-permute-start(f32[1,1,7,2,128,128]{5,4,3,2,1,0:T(8,128)S(1)} %bitcast_subtract_fusion.2), channel_id=1, source_target_pairs={{16,0},{32,16},{48,32},{64,48},{80,64},{96,80},{112,96},{128,112},... | collective-permute-start | bytes 2752520 | tf_op jit(solution)/shard_map/ppermute | solution.py:26
  632.4 114.1 %collective-permute-start.16 = (f32[1,1,7,2,128,128]{5,4,3,2,1,0:T(8,128)S(1)}, f32[1,1,7,2,128,128]{5,4,3,2,1,0:T(8,128)}, u32[]{:S(2)}, u32[]{:S(2)}) collective-permute-start(f32[1,1,7,2,128,128]{5,4,3,2,1,0:T(8,128)S(1)} %bitcast_subtract_fusion.2), channel_id=1, source_target_pairs={{0,1},{1,2},{2,3},{3,4},{4,5},{5,6},{6,7},{7,8},{8,9},{9,10},{10,1... | collective-permute-start | bytes 2752520 | tf_op jit(solution)/shard_map/ppermute | solution.py:23
  632.5 114.1 %collective-permute-start.17 = (f32[1,1,7,2,128,128]{5,4,3,2,1,0:T(8,128)S(1)}, f32[1,1,7,2,128,128]{5,4,3,2,1,0:T(8,128)}, u32[]{:S(2)}, u32[]{:S(2)}) collective-permute-start(f32[1,1,7,2,128,128]{5,4,3,2,1,0:T(8,128)S(1)} %bitcast_subtract_fusion.2), channel_id=1, source_target_pairs={{1,0},{2,1},{3,2},{4,3},{5,4},{6,5},{7,6},{8,7},{9,8},{10,9},{11,1... | collective-permute-start | bytes 2752520 | tf_op jit(solution)/shard_map/ppermute | solution.py:26
  825.9 43.6 %collective-permute-start.22 = (f32[1,1,7,2,128,128]{5,4,3,2,1,0:T(8,128)}, f32[1,1,7,2,128,128]{5,4,3,2,1,0:T(8,128)S(1)}, u32[]{:S(2)}, u32[]{:S(2)}) collective-permute-start(f32[1,1,7,2,128,128]{5,4,3,2,1,0:T(8,128)} %bitcast_subtract_fusion.1), channel_id=1, source_target_pairs={{0,16},{16,32},{32,48},{48,64},{64,80},{80,96},{96,112},{112,128},... | collective-permute-start | bytes 2752520 | tf_op jit(solution)/shard_map/ppermute | solution.py:23
  825.9 43.6 %collective-permute-start.23 = (f32[1,1,7,2,128,128]{5,4,3,2,1,0:T(8,128)}, f32[1,1,7,2,128,128]{5,4,3,2,1,0:T(8,128)S(1)}, u32[]{:S(2)}, u32[]{:S(2)}) collective-permute-start(f32[1,1,7,2,128,128]{5,4,3,2,1,0:T(8,128)} %bitcast_subtract_fusion.1), channel_id=1, source_target_pairs={{16,0},{32,16},{48,32},{64,48},{80,64},{96,80},{112,96},{128,112},... | collective-permute-start | bytes 2752520 | tf_op jit(solution)/shard_map/ppermute | solution.py:26
  830.3 109.5 %collective-permute-start.20 = (f32[1,1,7,2,128,128]{5,4,3,2,1,0:T(8,128)}, f32[1,1,7,2,128,128]{5,4,3,2,1,0:T(8,128)}, u32[]{:S(2)}, u32[]{:S(2)}) collective-permute-start(f32[1,1,7,2,128,128]{5,4,3,2,1,0:T(8,128)} %bitcast_subtract_fusion.1), channel_id=1, source_target_pairs={{0,1},{1,2},{2,3},{3,4},{4,5},{5,6},{6,7},{7,8},{8,9},{9,10},{10,1... | collective-permute-start | bytes 2752520 | tf_op jit(solution)/shard_map/ppermute | solution.py:23
  830.6 109.2 %collective-permute-start.21 = (f32[1,1,7,2,128,128]{5,4,3,2,1,0:T(8,128)}, f32[1,1,7,2,128,128]{5,4,3,2,1,0:T(8,128)}, u32[]{:S(2)}, u32[]{:S(2)}) collective-permute-start(f32[1,1,7,2,128,128]{5,4,3,2,1,0:T(8,128)} %bitcast_subtract_fusion.1), channel_id=1, source_target_pairs={{1,0},{2,1},{3,2},{4,3},{5,4},{6,5},{7,6},{8,7},{9,8},{10,9},{11,1... | collective-permute-start | bytes 2752520 | tf_op jit(solution)/shard_map/ppermute | solution.py:26
  939.8 4.0 copy-start.5
where the time goes:
time: 1030 us; the launch traced here: 1010 us
  local copies, waits for them, and re-layouts  404 us (39%)
  waiting for transfers between devices  220 us (21%)
  loops' own time  126 us (12%)
  matrix products  90.8 us (9%)
  other arithmetic  64.9 us (6%)
  starting transfers between devices  63.3 us (6%)
  blocking collectives  40.6 us (4%)
    ppermute x12, waiting for transfers between devices, with_halo(): lax.ppermute(lax.slice_in_dim(block, block.shape[dim] - width, None, axis...  186 us
    gather x63, local copies, waits for them, and re-layouts, one_target(): right_part = right_rim[row_pick[:, None], partners_row[:, None], layer_pick]  153 us
    gather x63, local copies, waits for them, and re-layouts, one_target(): left_rim[col_pick[partners_row], left_slots]  151 us
    another operation x9, loops' own time, sparse_product(): return lax.map(one_target, jnp.arange(count_offsets, dtype=jnp.int32))  126 us
    dot_general x63, matrix products, one_target(): jnp.einsum('tsab,tsbc->sac', left_part, right_part, precision=FULL_PRECIS...  90.8 us
    ppermute x12, starting transfers between devices, with_halo(): lax.ppermute(lax.slice_in_dim(block, 0, width, axis=dim), axis, backward)  53.8 us
    psum x5, blocking collectives, one_axis_at_a_time(): return functools.reduce(lax.psum, axes, array)  40.6 us
    gather x63, local copies, waits for them, and re-layouts, one_target(): col_pick[partners_row]  40.5 us
  transfers between devices with their start and end apart: 24, of which 11 were waited for; matrix products, arithmetic and copies ran while one was open for 19% of the time, Pallas kernels for 0%

commit v1 on v0

v1 whole, which is shorter than its diff:
```python
import functools

import jax
import jax.numpy as jnp
from jax import lax
from jax.experimental import pallas as pl
from jax.experimental.pallas import tpu as pltpu
from jax.sharding import PartitionSpec as P

ROW, COL = "row", "col"
MESH_ID = pl.DeviceIdType.MESH
F32, BF16, I32 = jnp.float32, jnp.bfloat16, jnp.int32
B = 128

X0, X1, X2, HAM, G2, G1, X3, G0 = range(8)


def split(value):
    high = value.astype(BF16)
    return high, (value - high.astype(F32)).astype(BF16)


def fold(r):
    return (r[:B, :B] + r[B:, B:]) + (r[:B, B:] + r[B:, :B])


def dot(a, b, dims):
    return lax.dot_general(a, b, (dims, ((), ())), preferred_element_type=F32)


def cat(parts, axis):
    return jnp.concatenate(parts, axis=axis)


def dot_nn(lefts, rights):
    lhs = cat([cat([h for h, _ in lefts], 1), cat([l for _, l in lefts], 1)], 0)
    rhs = cat([cat([h, l], 1) for h, l in rights], 0)
    return fold(dot(lhs, rhs, ((1,), (0,))))


def dot_tn(left, right):
    return fold(dot(cat(left, 1), cat(right, 1), ((0,), (0,))))


def dot_nt(left, right):
    return fold(dot(cat(left, 0), cat(right, 0), ((1,), (1,))))


def gram(high, low):
    return dot(high, cat([high, low], 1), ((0,), (0,)))


def total(conditions, values):
    return functools.reduce(lambda a, b: a + b, [jnp.where(c, v, 0) for c, v in zip(conditions, values)])


def kernel(
    eta, n_row, n_col, order,
    off_ref, branch_ref, x_hbm, h_hbm,
    new_hbm, grad_hbm, tot_ref,
    raw_x, raw_h, cf, eh, el, dh, dl, rd, sp, rp, ow, ox, rx, ar_src, ar, out_new, out_grad, tab,
    in_sem, out_sem, d_send, d_recv, p_send, p_recv, x_send, x_recv, ar_send, ar_recv,
):
    p, q = lax.axis_index(ROW), lax.axis_index(COL)
    up, down = lax.rem(p + 1, n_row), lax.rem(p + n_row - 1, n_row)
    right, left = lax.rem(q + 1, n_col), lax.rem(q + n_col - 1, n_col)

    loads = [
        pltpu.make_async_copy(x_hbm.at[0, 0], raw_x, in_sem.at[0]),
        pltpu.make_async_copy(h_hbm.at[0, 0], raw_h, in_sem.at[1]),
    ]
    for load in loads:
        load.start()

    barrier = pltpu.get_barrier_semaphore()

    def greet_row(d, carry):
        pl.semaphore_signal(barrier, inc=1, device_id=(lax.rem(p + d, n_row), q), device_id_type=MESH_ID)
        return carry

    def greet_col(d, carry):
        pl.semaphore_signal(barrier, inc=1, device_id=(p, lax.rem(q + d, n_col)), device_id_type=MESH_ID)
        return carry

    lax.fori_loop(1, n_row, greet_row, 0)
    lax.fori_loop(1, n_col, greet_col, 0)
    greeted = n_row + n_col - 2
    if eta:
        corners = [(up, left if eta > 0 else right), (down, right if eta > 0 else left)]
        for corner in corners:
            pl.semaphore_signal(barrier, inc=1, device_id=corner, device_id_type=MESH_ID)
        greeted += 2

    off = [[off_ref[t, c] for c in range(3)] for t in range(7)]
    lay = [lax.rem(o[2] + 2, 2) for o in off]
    zero = [(o[0] == 0) & (o[1] == 0) & (s == 0) for o, s in zip(off, lay)]
    slots = [total(zero, range(7))]
    steps = [(0, 0, 0)]
    if eta:
        firsts = [[(o[0] == a) & (o[1] == b) for o in off] for a, b in ((1, 0), (0, eta), (1, eta))]
    else:
        lead = [(o[0] == 1) | ((o[0] == 0) & (o[1] == 1)) for o in off]
        before, count = [], jnp.int32(0)
        for is_lead in lead:
            before.append(count)
            count = count + jnp.where(is_lead, 1, 0)
        firsts = [[is_lead & (b == j) for is_lead, b in zip(lead, before)] for j in range(3)]
    for first in firsts:
        a, b, s = total(first, [o[0] for o in off]), total(first, [o[1] for o in off]), total(first, lay)
        mirror = [(o[0] == -a) & (o[1] == -b) & (t == s) for o, t in zip(off, lay)]
        slots += [total(first, range(7)), total(mirror, range(7))]
        steps += [(a, b, s), (-a, -b, s)]
    for k in range(7):
        tab[0, k] = jnp.clip(slots[k], 0, 6)
        for c in range(3):
            tab[1 + c, k] = jnp.clip(jnp.int32(0) + steps[k][c], -1, 1)
    for t in range(7):
        tab[4, t] = jnp.clip(total([slots[k] == t for k in range(7)], range(7)), 0, 6)
    signs = [(2 * branch_ref[k] - 1).astype(F32) for k in range(3)]
    keep = [jnp.where(steps[1 + 2 * j][0] != 0, 1.0, 0.0).astype(F32) for j in range(3)]

    def take_in(which, x):
        loads[which].wait()
        raw = (raw_x, raw_h)[which]

        def body(k, carry):
            slot = tab[0, k]
            cf[x, k] = raw[slot]
            return carry

        lax.fori_loop(0, 7, body, 0)

    def split_edges(x):
        def body(i, carry):
            for s in range(2):
                eh[x, i, s], el[x, i, s] = split(cf[x, i + 1, s])
            return carry

        lax.fori_loop(0, 6, body, 0)

    def split_diagonal(x):
        for s in range(2):
            high, low = split(cf[x, 0, s])
            for place in (1, 4):
                dh[x, place, s], dl[x, place, s] = high, low

    def diagonal_copies(x):
        targets = ((p, right), (p, left), (up, q), (down, q))
        return [
            pltpu.make_async_remote_copy(
                src_ref=cf.at[x, 0],
                dst_ref=rd.at[x, i],
                send_sem=d_send.at[x, i],
                recv_sem=d_recv.at[x, i],
                device_id=target,
                device_id_type=MESH_ID,
            )
            for i, target in enumerate(targets)
        ]

    def send_diagonal(x):
        for copy in diagonal_copies(x):
            copy.start()

    def receive_diagonal(x):
        for i, copy in enumerate(diagonal_copies(x)):
            copy.wait_recv()
            for s in range(2):
                place = (0, 2, 3, 5)[i]
                dh[x, place, s], dl[x, place, s] = split(rd[x, i, s])

    def partial_copies(n):
        return [
            pltpu.make_async_remote_copy(
                src_ref=sp.at[n, g],
                dst_ref=rp.at[n, g],
                send_sem=p_send.at[n, g],
                recv_sem=p_recv.at[n, g],
                device_id=((up, q), (down, q))[g],
                device_id_type=MESH_ID,
            )
            for g in range(2)
        ]

    def corner_copies(n):
        copies = []
        for j in range(3):
            for g in range(2):
                row_to = (up, down)[g]
                col_to = (left, right)[g] if eta > 0 else (right, left)[g]
                target = ((row_to, q), (p, col_to), (row_to, col_to))[j]
                copies.append(
                    pltpu.make_async_remote_copy(
                        src_ref=ox.at[n, j, g],
                        dst_ref=rx[n].at[j, 1 - g],
                        send_sem=x_send.at[n, 2 * j + g],
                        recv_sem=x_recv.at[n, 2 * j + g],
                        device_id=target,
                        device_id_type=MESH_ID,
                    )
                )
        return copies

    def edge(x, k, s):
        return eh[x, k - 1, s], el[x, k - 1, s]

    def send_partials(n, x, g=None):
        def body(s, carry):
            own = None
            for sign in range(2):
                sent = None
                for j in range(3):
                    k = 1 + 2 * j + sign
                    source = lax.rem(s + tab[3, k], 2)
                    if g is None:
                        r = gram(*edge(x, k, source))
                    else:
                        r = dot_tn(edge(g, k, source), edge(x, k, source))
                    away = r * keep[j]
                    stay = r - away
                    sent = away if sent is None else sent + away
                    own = stay if own is None else own + stay
                if g is None:
                    sp[n, sign, s] = sent[:, :B] + sent[:, B:] + sent[:, B:].T
                else:
                    sp[n, sign, s] = sent + sent.T
            if g is None:
                own = own + gram(dh[x, 1, s], dl[x, 1, s])
                ow[n, s] = own[:, :B] + own[:, B:] + own[:, B:].T
            else:
                own = own + dot_nn([(dh[g, 1, s], dl[g, 1, s])], [(dh[x, 1, s], dl[x, 1, s])])
                ow[n, s] = own + own.T
            return carry

        lax.fori_loop(0, 2, body, 0)
        for copy in partial_copies(n):
            copy.start()
        if not eta:
            return

        def corners_body(i, carry):
            sign, s = i // 2, lax.rem(i, 2)
            other = lax.rem(s + steps[3][2], 2)
            pairs = [(x, x)] if g is None else [(g, x), (x, g)]
            ka, kb, kc = 1 + sign, 3 + sign, 5 + sign
            ox[n, 0, sign, s] = functools.reduce(
                jnp.add, [dot_tn(edge(u, kb, s), edge(v, kc, s)) for u, v in pairs]
            )
            ox[n, 1, sign, s] = functools.reduce(
                jnp.add, [dot_nt(edge(u, kc, s), edge(v, ka, other)) for u, v in pairs]
            )
            ox[n, 2, sign, s] = functools.reduce(
                jnp.add, [dot_nn([edge(u, kb, s)], [edge(v, ka, other)]) for u, v in pairs]
            )
            return carry

        lax.fori_loop(0, 4, corners_body, 0)
        for copy in corner_copies(n):
            copy.start()

    def update_edges(n, sign, x, out, g=None, excess=None):
        base = x if g is None else g
        if eta:
            for copy in corner_copies(n):
                copy.wait_recv()
        lb = steps[3][2]
        lc = steps[5][2]

        def body(i, carry):
            k = i + 1
            to_left, to_right = 1 - tab[2, k], 4 + tab[1, k]
            for s in range(2):
                t = lax.rem(s + tab[3, k], 2)

                def near(m):
                    return (dh[m, to_left, s], dl[m, to_left, s]), (dh[m, to_right, t], dl[m, to_right, t])

                x_left, x_right = near(x)
                x_edge = (eh[x, i, s], el[x, i, s])
                if g is None:
                    product = dot_nn([x_left, x_edge], [x_edge, x_right])
                else:
                    g_left, g_right = near(g)
                    g_edge = (eh[g, i, s], el[g, i, s])
                    product = dot_nn([g_left, x_left, g_edge, x_edge], [x_edge, g_edge, x_right, g_right])
                if eta:
                    j, sg = i // 2, lax.rem(i, 2)
                    mine = jnp.where(j == 0, lb, 0)
                    theirs = jnp.where(j == 1, lb, lc)
                    product = product + ox[n, j, sg, lax.rem(s + mine, 2)] + rx[n][j, sg, lax.rem(s + theirs, 2)].T
                value = (1.0 + sign) * cf[base, k, s] - sign * product
                if excess is not None:
                    value = value - (2.0 * sign * excess) * cf[x, k, s]
                cf[out, k, s] = value
                if out < X3:
                    eh[out, i, s], el[out, i, s] = split(value)
            return carry

        lax.fori_loop(0, 6, body, 0)

    eye = lax.broadcasted_iota(I32, (B, B), 0) == lax.broadcasted_iota(I32, (B, B), 1)

    def update_diagonal(n, sign, x, out, g=None, excess=None):
        base = x if g is None else g
        for copy in partial_copies(n):
            copy.wait_recv()
        for s in range(2):
            product = ow[n, s] + rp[n, 0, s] + rp[n, 1, s]
            value = (1.0 + sign) * cf[base, 0, s] - sign * product
            if excess is not None:
                value = value + jnp.where(eye, (1.0 + sign) * excess, 0.0) - (2.0 * sign * excess) * cf[x, 0, s]
            cf[out, 0, s] = value
        if out < X3:
            split_diagonal(out)
            send_diagonal(out)

    def reduce_copy(turn, stage, d):
        return pltpu.make_async_remote_copy(
            src_ref=ar_src.at[turn, stage],
            dst_ref=ar.at[turn, stage, d],
            send_sem=ar_send.at[turn, stage, d],
            recv_sem=ar_recv.at[turn, stage, d],
            device_id=(lax.rem(p + d, n_row), q) if stage == 0 else (p, lax.rem(q + d, n_col)),
            device_id_type=MESH_ID,
        )

    def reduce_start(turn, stage, value):
        ar_src[turn, stage] = value

        def body(d, carry):
            reduce_copy(turn, stage, d).start()
            return carry

        lax.fori_loop(1, (n_row, n_col)[stage], body, 0)

    def reduce_end(turn, stage):
        count = (n_row, n_col)[stage]

        def wait(d, carry):
            reduce_copy(turn, stage, d).wait_recv()
            return carry

        lax.fori_loop(1, count, wait, 0)
        return lax.fori_loop(1, count, lambda d, v: v + ar[turn, stage, d], ar_src[turn, stage])

    def tiles(value):
        return jnp.sum(value.reshape(-1, 8, B), axis=0)

    def trace_of(x):
        return functools.reduce(jnp.add, [tiles(jnp.where(eye, cf[x, 0, s], 0.0)) for s in range(2)])

    def dot_all(a, b):
        def body(k, carry):
            return carry + tiles(cf[a, k] * cf[b, k])

        return lax.fori_loop(0, 7, body, jnp.zeros((8, B), F32))

    def put_out(x, which, hbm):
        out_buf = (out_new, out_grad)[which]
        def body(t, carry):
            slot = tab[4, t]
            out_buf[t] = cf[x, slot]
            return carry

        lax.fori_loop(0, 7, body, 0)
        copy = pltpu.make_async_copy(out_buf, hbm.at[0, 0], out_sem.at[which])
        copy.start()
        return copy

    take_in(0, X0)
    pl.semaphore_wait(barrier, greeted)
    send_diagonal(X0)
    split_edges(X0)
    split_diagonal(X0)
    send_partials(0, X0)
    take_in(1, HAM)
    send_diagonal(HAM)
    split_edges(HAM)
    split_diagonal(HAM)
    for n in range(2):
        if n:
            send_partials(n, n)
        update_diagonal(n, signs[n], n, n + 1)
        receive_diagonal(n)
        update_edges(n, signs[n], n, n + 1)
    last = signs[2]
    send_partials(3, X2, HAM)
    occupied = (1.0 + last) * trace_of(X2) - last * dot_all(X2, X2)
    reduce_start(0, 0, jnp.stack([occupied, occupied]))
    send_partials(2, X2)
    reduce_start(0, 1, reduce_end(0, 0))
    receive_diagonal(HAM)
    receive_diagonal(X2)
    excess = jnp.sum(reduce_end(0, 1)[0]) / order - 0.5
    update_diagonal(3, last, X2, G2, HAM, excess)
    update_edges(3, last, X2, G2, HAM, excess)
    send_partials(4, X1, G2)
    update_diagonal(2, last, X2, X3)
    update_edges(2, last, X2, X3)
    reduce_start(1, 0, jnp.stack([dot_all(HAM, X3), trace_of(X3)]))
    first_out = put_out(X3, 0, new_hbm)
    update_diagonal(4, signs[1], X1, G1, G2)
    receive_diagonal(G2)
    update_edges(4, signs[1], X1, G1, G2)
    send_partials(5, X0, G1)
    reduce_start(1, 1, reduce_end(1, 0))
    update_diagonal(5, signs[0], X0, G0, G1)
    receive_diagonal(G1)
    update_edges(5, signs[0], X0, G0, G1)
    second_out = put_out(G0, 1, grad_hbm)
    sums = reduce_end(1, 1)
    tot_ref[0] = jnp.sum(sums[0]) / order
    tot_ref[1] = jnp.sum(sums[1]) / order

    for x in range(6):
        for copy in diagonal_copies(x) + partial_copies(x) + (corner_copies(x) if eta else []):
            copy.wait_send()
    for turn in range(2):
        for stage in range(2):

            def wait(d, carry):
                reduce_copy(turn, stage, d).wait_send()
                return carry

            lax.fori_loop(1, (n_row, n_col)[stage], wait, 0)
    first_out.wait()
    second_out.wait()


def call(eta, n_row, n_col, density, hamiltonian, offsets, branch):
    blocks = density.shape[2:]
    order = float(n_row * n_col * blocks[1] * blocks[2])
    extra = 6 if eta else 1
    any_space = pl.BlockSpec(memory_space=pl.ANY)
    smem = pl.BlockSpec(memory_space=pltpu.SMEM)
    dma = pltpu.SemaphoreType.DMA
    width = max(n_row, n_col)
    return pl.pallas_call(
        functools.partial(kernel, eta, n_row, n_col, order),
        out_shape=(
            jax.ShapeDtypeStruct(density.shape, F32),
            jax.ShapeDtypeStruct(density.shape, F32),
            jax.ShapeDtypeStruct((2,), F32),
        ),
        in_specs=[smem, smem, any_space, any_space],
        out_specs=(any_space, any_space, smem),
        scratch_shapes=[
            pltpu.VMEM((7, 2, B, B), F32),
            pltpu.VMEM((7, 2, B, B), F32),
            pltpu.VMEM((8, 7, 2, B, B), F32),
            pltpu.VMEM((6, 6, 2, B, B), BF16),
            pltpu.VMEM((6, 6, 2, B, B), BF16),
            pltpu.VMEM((6, 6, 2, B, B), BF16),
            pltpu.VMEM((6, 6, 2, B, B), BF16),
            pltpu.VMEM((6, 4, 2, B, B), F32),
            pltpu.VMEM((6, 2, 2, B, B), F32),
            pltpu.VMEM((6, 2, 2, B, B), F32),
            pltpu.VMEM((6, 2, B, B), F32),
            pltpu.VMEM((extra, 3, 2, 2, B, B), F32),
            [pltpu.VMEM((3, 2, 2, B, B), F32)] * extra,
            pltpu.VMEM((2, 2, 2, 8, B), F32),
            pltpu.VMEM((2, 2, width, 2, 8, B), F32),
            pltpu.VMEM((7, 2, B, B), F32),
            pltpu.VMEM((7, 2, B, B), F32),
            pltpu.SMEM((5, 8), I32),
            dma((2,)),
            dma((2,)),
            dma((6, 4)),
            dma((6, 4)),
            dma((6, 2)),
            dma((6, 2)),
            dma((6, 6)),
            dma((6, 6)),
            dma((2, 2, width)),
            dma((2, 2, width)),
        ],
        compiler_params=pltpu.CompilerParams(
            collective_id=1 + eta, has_side_effects=True, vmem_limit_bytes=56 * 1024 * 1024
        ),
        name="sp2_" + ("mirrored", "open", "closed")[1 + eta],
    )(offsets, branch, density, hamiltonian)


def pattern_class(offsets):
    rows, cols = offsets[:, 0], offsets[:, 1]
    layers = offsets[:, 2] % 2

    def find(a, b):
        here = (rows == a) & (cols == b)
        return jnp.any(here), jnp.sum(jnp.where(here, layers, 0))

    has_a, layer_a = find(1, 0)
    has_b, layer_b = find(0, 1)
    has_c, layer_c = find(1, 1)
    has_d, layer_d = find(1, -1)
    pair = has_a & has_b
    plus = pair & has_c & ((layer_a + layer_b + layer_c) % 2 == 0)
    minus = pair & has_d & ((layer_a + layer_b + layer_d) % 2 == 0)
    return jnp.where(plus, 1, jnp.where(minus, 2, 0)).astype(I32)


def solution(mesh):
    n_row, n_col = mesh.shape[ROW], mesh.shape[COL]

    def local(density, hamiltonian, offsets, branch):
        branches = [functools.partial(call, eta, n_row, n_col) for eta in (0, 1, -1)]
        return lax.switch(pattern_class(offsets), branches, density, hamiltonian, offsets, branch)

    spec = P(ROW, COL, None, None, None, None)
    return jax.shard_map(
        local, mesh=mesh, in_specs=(spec, spec, P(), P()), out_specs=(spec, spec, P()), check_vma=False
    )
```

time: 1030 us -> 103 us (0.10); the launches traced: 1010 us -> 102 us
  local copies, waits for them, and re-layouts: 404 us -> 4.37 us
  waiting for transfers between devices: 220 us -> 0 us
  loops' own time: 126 us -> 0.23 us
  matrix products: 90.8 us -> 0 us
  Pallas kernels: 0 us -> 87.8 us
  starting transfers between devices: 63.3 us -> 0 us
  other arithmetic: 64.9 us -> 4.06 us
  blocking collectives: 40.6 us -> 0 us
    gather x189 -> x0, local copies, waits for them, and re-layouts: 344 us -> none  [the longest x63 153 us: one_target(): right_part = right_rim[row_pick[:, None], partners_row[:, None], layer_pick]]
    ppermute x24 -> x0, waiting for transfers between devices: 220 us -> none  [the longest x12 186 us: with_halo(): lax.ppermute(lax.slice_in_dim(block, block.shape[dim] - width, None, axis...]
    another operation x9 -> x1, loops' own time: 126 us -> 0.23 us  [local(): lax.switch(pattern_class(offsets), branches, density, hamiltonian, offset...]
    dot_general x63 -> x0, matrix products: 90.8 us -> none  [one_target(): jnp.einsum('tsab,tsbc->sac', left_part, right_part, precision=FULL_PRECIS...]
    pallas_call x0 -> x1, Pallas kernels: none -> 87.8 us  [call(): pl.pallas_call(functools.partial(kernel, eta, n_row, n_col, order), out_s...]
    ppermute x24 -> x0, starting transfers between devices: 63.3 us -> none  [the longest x12 53.8 us: with_halo(): lax.ppermute(lax.slice_in_dim(block, 0, width, axis=dim), axis, backward)]
    psum x5 -> x0, blocking collectives: 40.6 us -> none  [one_axis_at_a_time(): return functools.reduce(lax.psum, axes, array)]
    dynamic_slice x63 -> x0, local copies, waits for them, and re-layouts: 39.1 us -> none  [sparse_product(): return lax.map(one_target, jnp.arange(count_offsets, dtype=jnp.int32))]
  transfers between devices with their start and end apart: 24 -> 0, of which waited for: 11 -> 0; matrix products, arithmetic and copies ran while one was open for 19% -> 0% of each run, Pallas kernels for 0% -> 0%
where the time goes in v1:
time: 103 us; the launch traced here: 102 us
  Pallas kernels  87.8 us (85%)
  between operations  5.85 us (6%)
  local copies, waits for them, and re-layouts  4.37 us (4%)
  other arithmetic  4.06 us (4%)
    pallas_call x1, Pallas kernels, call(): pl.pallas_call(functools.partial(kernel, eta, n_row, n_col, order), out_s...  87.8 us
    unnamed x7, local copies, waits for them, and re-layouts  3.69 us
    reduce_or x4, other arithmetic, find(): return (jnp.any(here), jnp.sum(jnp.where(here, layers, 0)))  3.31 us

profile of v1, /device:TPU:32, one launch (start us, length us, event | category | flops | bytes accessed | tf_op | source)
XLA Modules:
  0.0 102.3 jit_solution(13299282582504105102)
XLA Ops:
  0.6 1.4 %fusion.5 = (pred[]{:T(512)}, pred[7,1]{0,1:T(4,128)(4,1)S(1)}) fusion(s32[7,3]{0,1:T(4,128)} %param.9), kind=kLoop, calls=%fused_computation.17 | loop fusion | flops 27 | bytes 64 | tf_op jit(solution)/shard_map/reduce_or | solution.py:490
  2.0 0.0 copy-start
  2.0 0.7 copy-done
  2.7 0.8 fusion.3
  6.0 0.6 reduce_or.36
  6.7 0.6 reduce_or.37
  9.3 0.6 reduce_or.38
  10.6 0.0 copy-start.1
  10.6 0.6 copy-done.1
  11.2 88.7 %conditional.1 = ((f32[1,1,7,2,128,128]{5,4,3,2,1,0:T(8,128)S(1)}, f32[1,1,7,2,128,128]{5,4,3,2,1,0:T(8,128)S(1)}, f32[2]{0:T(128)S(1)})) conditional(s32[]{:T(128)} %clamp.3, (s32[7,3]{0,1:T(4,128)S(1)}, s32[3]{0:T(128)S(1)}, f32[1,1,7,2,128,128]{5,4,3,2,1,0:T(8,128)}, f32[1,1,7,2,128,128]{5,4,3,2,1,0:T(8,128)}) %tuple.47, ...), branch_computations={%region_8.9_spmd, %region_9.10_spmd, %region_10.11_spmd} | conditional | bytes 176 | solution.py:507
  11.2 0.7 copy.16.off_ref
  11.9 87.8 %sp2_open.1 = (f32[1,1,7,2,128,128]{5,4,3,2,1,0:T(8,128)S(1)}, f32[1,1,7,2,128,128]{5,4,3,2,1,0:T(8,128)S(1)}, f32[2]{0:T(128)S(1)}) custom-call(s32[7,3]{1,0:T(8,128)} %copy.16.off_ref, s32[3]{0:T(128)S(1)} %get-tuple-element.25.branch_ref, f32[1,1,7,2,128,128]{5,4,3,2,1,0:T(8,128)} %get-tuple-element.26.x_hbm, ...), custom_call_target="tpu_custom_call" | custom-call | tf_op jit(solution)/shard_map/cond/branch_0_fun/sp2_open/pallas_call | solution.py:438
  99.9 0.9 copy.31
  100.8 0.9 copy.32
  101.8 0.5 copy.33
Async XLA Ops:
  2.0 0.7 copy-start
  10.6 0.7 copy-start.1

commit v2 on v1

--- a/solution.py
+++ b/solution.py
@@ -11,6 +11,7 @@
 MESH_ID = pl.DeviceIdType.MESH
 F32, BF16, I32 = jnp.float32, jnp.bfloat16, jnp.int32
 B = 128
+PACKED = B + 8
 
 X0, X1, X2, HAM, G2, G1, X3, G0 = range(8)
 
@@ -57,13 +58,26 @@
 def kernel(
     eta, n_row, n_col, order,
     off_ref, branch_ref, x_hbm, h_hbm,
-    new_hbm, grad_hbm, tot_ref,
-    raw_x, raw_h, cf, eh, el, dh, dl, rd, sp, rp, ow, ox, rx, ar_src, ar, out_new, out_grad, tab,
-    in_sem, out_sem, d_send, d_recv, p_send, p_recv, x_send, x_recv, ar_send, ar_recv,
+    new_ref, grad_ref, tot_ref,
+    raw_x, raw_h, cf, eh, el, dh, dl, sd, rd, parts, sp, rp, ow, ox, rx, ar_src, ar, tab,
+    in_sem, d_send, d_recv, p_send, p_recv, x_send, x_recv, ar_send, ar_recv,
 ):
     p, q = lax.axis_index(ROW), lax.axis_index(COL)
     up, down = lax.rem(p + 1, n_row), lax.rem(p + n_row - 1, n_row)
     right, left = lax.rem(q + 1, n_col), lax.rem(q + n_col - 1, n_col)
+
+    row_id = lax.broadcasted_iota(I32, (B, B), 0)
+    col_id = lax.broadcasted_iota(I32, (B, B), 1)
+    eye, lower = row_id == col_id, row_id >= col_id
+
+    def pack(ref, first, second):
+        ref[0:B, :] = jnp.where(lower, first, second)
+        ref[B : B + 1, :] = jnp.sum(jnp.where(eye, second, 0.0), axis=0, keepdims=True)
+
+    def unpack(both, diagonal):
+        flipped = both.T
+        second = jnp.where(lower, flipped, both)
+        return jnp.where(lower, both, flipped), jnp.where(eye, diagonal, second)
 
     loads = [
         pltpu.make_async_copy(x_hbm.at[0, 0], raw_x, in_sem.at[0]),
@@ -148,7 +162,7 @@
         targets = ((p, right), (p, left), (up, q), (down, q))
         return [
             pltpu.make_async_remote_copy(
-                src_ref=cf.at[x, 0],
+                src_ref=sd.at[x],
                 dst_ref=rd.at[x, i],
                 send_sem=d_send.at[x, i],
                 recv_sem=d_recv.at[x, i],
@@ -159,15 +173,18 @@
         ]
 
     def send_diagonal(x):
+        pack(sd.at[x], cf[x, 0, 0], cf[x, 0, 1])
         for copy in diagonal_copies(x):
             copy.start()
 
-    def receive_diagonal(x):
+    def receive_diagonal(x, extra=None):
         for i, copy in enumerate(diagonal_copies(x)):
             copy.wait_recv()
-            for s in range(2):
-                place = (0, 2, 3, 5)[i]
-                dh[x, place, s], dl[x, place, s] = split(rd[x, i, s])
+            place = (0, 2, 3, 5)[i]
+            for s, value in enumerate(unpack(rd[x, i, 0:B, :], rd[x, i, B : B + 1, :])):
+                if extra is not None:
+                    value = value + extra(dh[X2, place, s].astype(F32) + dl[X2, place, s].astype(F32))
+                dh[x, place, s], dl[x, place, s] = split(value)
 
     def partial_copies(n):
         return [
@@ -221,9 +238,9 @@
                     sent = away if sent is None else sent + away
                     own = stay if own is None else own + stay
                 if g is None:
-                    sp[n, sign, s] = sent[:, :B] + sent[:, B:] + sent[:, B:].T
+                    parts[sign, s] = sent[:, :B] + sent[:, B:] + sent[:, B:].T
                 else:
-                    sp[n, sign, s] = sent + sent.T
+                    parts[sign, s] = sent + sent.T
             if g is None:
                 own = own + gram(dh[x, 1, s], dl[x, 1, s])
                 ow[n, s] = own[:, :B] + own[:, B:] + own[:, B:].T
@@ -233,7 +250,8 @@
             return carry
 
         lax.fori_loop(0, 2, body, 0)
-        for copy in partial_copies(n):
+        for sign, copy in enumerate(partial_copies(n)):
+            pack(sp.at[n, sign], parts[sign, 0], parts[sign, 1])
             copy.start()
         if not eta:
             return
@@ -258,10 +276,10 @@
         for copy in corner_copies(n):
             copy.start()
 
-    def update_edges(n, sign, x, out, g=None, excess=None):
+    def update_edges(n, sign, x, out, g=None, extra=None):
         base = x if g is None else g
         if eta:
-            for copy in corner_copies(n):
+            for copy in corner_copies(n) + (corner_copies(6) if extra is not None else []):
                 copy.wait_recv()
         lb = steps[3][2]
         lc = steps[5][2]
@@ -287,10 +305,12 @@
                     j, sg = i // 2, lax.rem(i, 2)
                     mine = jnp.where(j == 0, lb, 0)
                     theirs = jnp.where(j == 1, lb, lc)
-                    product = product + ox[n, j, sg, lax.rem(s + mine, 2)] + rx[n][j, sg, lax.rem(s + theirs, 2)].T
+                    corner = ox[n, j, sg, lax.rem(s + mine, 2)] + rx[n][j, sg, lax.rem(s + theirs, 2)].T
+                    product = product + corner
+                    if extra is not None:
+                        corner = ox[6, j, sg, lax.rem(s + mine, 2)] + rx[6][j, sg, lax.rem(s + theirs, 2)].T
+                        product = product + extra * corner
                 value = (1.0 + sign) * cf[base, k, s] - sign * product
-                if excess is not None:
-                    value = value - (2.0 * sign * excess) * cf[x, k, s]
                 cf[out, k, s] = value
                 if out < X3:
                     eh[out, i, s], el[out, i, s] = split(value)
@@ -298,18 +318,19 @@
 
         lax.fori_loop(0, 6, body, 0)
 
-    eye = lax.broadcasted_iota(I32, (B, B), 0) == lax.broadcasted_iota(I32, (B, B), 1)
-
-    def update_diagonal(n, sign, x, out, g=None, excess=None):
+    def update_diagonal(n, sign, x, out, g=None, extra=None):
         base = x if g is None else g
-        for copy in partial_copies(n):
+        for copy in partial_copies(n) + (partial_copies(6) if extra is not None else []):
             copy.wait_recv()
-        for s in range(2):
-            product = ow[n, s] + rp[n, 0, s] + rp[n, 1, s]
-            value = (1.0 + sign) * cf[base, 0, s] - sign * product
-            if excess is not None:
-                value = value + jnp.where(eye, (1.0 + sign) * excess, 0.0) - (2.0 * sign * excess) * cf[x, 0, s]
-            cf[out, 0, s] = value
+        arrived = rp[n, 0] + rp[n, 1]
+        if extra is not None:
+            one, same = extra
+            arrived = arrived + same * (rp[6, 0] + rp[6, 1])
+        for s, product in enumerate(unpack(arrived[0:B, :], arrived[B : B + 1, :])):
+            product = product + ow[n, s]
+            if extra is not None:
+                product = product + same * ow[6, s] + (2.0 * one) * cf[x, 0, s]
+            cf[out, 0, s] = (1.0 + sign) * cf[base, 0, s] - sign * product
         if out < X3:
             split_diagonal(out)
             send_diagonal(out)
@@ -355,17 +376,13 @@
 
         return lax.fori_loop(0, 7, body, jnp.zeros((8, B), F32))
 
-    def put_out(x, which, hbm):
-        out_buf = (out_new, out_grad)[which]
+    def put_out(x, ref):
         def body(t, carry):
             slot = tab[4, t]
-            out_buf[t] = cf[x, slot]
+            ref[0, 0, t] = cf[x, slot]
             return carry
 
         lax.fori_loop(0, 7, body, 0)
-        copy = pltpu.make_async_copy(out_buf, hbm.at[0, 0], out_sem.at[which])
-        copy.start()
-        return copy
 
     take_in(0, X0)
     pl.semaphore_wait(barrier, greeted)
@@ -374,46 +391,64 @@
     split_diagonal(X0)
     send_partials(0, X0)
     take_in(1, HAM)
-    send_diagonal(HAM)
     split_edges(HAM)
     split_diagonal(HAM)
-    for n in range(2):
-        if n:
-            send_partials(n, n)
-        update_diagonal(n, signs[n], n, n + 1)
-        receive_diagonal(n)
-        update_edges(n, signs[n], n, n + 1)
+    update_diagonal(0, signs[0], X0, X1)
+    receive_diagonal(X0)
+    update_edges(0, signs[0], X0, X1)
+    send_partials(1, X1)
+    send_diagonal(HAM)
+    update_diagonal(1, signs[1], X1, X2)
+    receive_diagonal(X1)
+    update_edges(1, signs[1], X1, X2)
     last = signs[2]
     send_partials(3, X2, HAM)
     occupied = (1.0 + last) * trace_of(X2) - last * dot_all(X2, X2)
     reduce_start(0, 0, jnp.stack([occupied, occupied]))
-    send_partials(2, X2)
+    send_partials(6, X1, X2)
     reduce_start(0, 1, reduce_end(0, 0))
+    update_diagonal(3, last, X2, G2, HAM)
     receive_diagonal(HAM)
     receive_diagonal(X2)
+    update_edges(3, last, X2, G2, HAM)
+    send_partials(4, X1, G2)
+    send_partials(2, X2)
     excess = jnp.sum(reduce_end(0, 1)[0]) / order - 0.5
-    update_diagonal(3, last, X2, G2, HAM, excess)
-    update_edges(3, last, X2, G2, HAM, excess)
-    send_partials(4, X1, G2)
+    one, same = (1.0 + last) * excess, -2.0 * last * excess
+
+    def complete(k, carry):
+        for s in range(2):
+            value = cf[G2, k, s] + same * cf[X2, k, s]
+            cf[G2, k, s] = value
+            eh[G2, k - 1, s], el[G2, k - 1, s] = split(value)
+        return carry
+
+    lax.fori_loop(1, 7, complete, 0)
+    for s in range(2):
+        cf[G2, 0, s] = cf[G2, 0, s] + jnp.where(eye, one, 0.0) + same * cf[X2, 0, s]
+    split_diagonal(G2)
+    update_diagonal(4, signs[1], X1, G1, G2, (one, same))
+    receive_diagonal(G2, lambda value: jnp.where(eye, one, 0.0) + same * value)
+    update_edges(4, signs[1], X1, G1, G2, same)
+    send_partials(5, X0, G1)
+    update_edges(2, last, X2, X3)
     update_diagonal(2, last, X2, X3)
-    update_edges(2, last, X2, X3)
     reduce_start(1, 0, jnp.stack([dot_all(HAM, X3), trace_of(X3)]))
-    first_out = put_out(X3, 0, new_hbm)
-    update_diagonal(4, signs[1], X1, G1, G2)
-    receive_diagonal(G2)
-    update_edges(4, signs[1], X1, G1, G2)
-    send_partials(5, X0, G1)
+    update_diagonal(5, signs[0], X0, G0, G1)
+    put_out(X3, new_ref)
     reduce_start(1, 1, reduce_end(1, 0))
-    update_diagonal(5, signs[0], X0, G0, G1)
     receive_diagonal(G1)
     update_edges(5, signs[0], X0, G0, G1)
-    second_out = put_out(G0, 1, grad_hbm)
+    put_out(G0, grad_ref)
     sums = reduce_end(1, 1)
     tot_ref[0] = jnp.sum(sums[0]) / order
     tot_ref[1] = jnp.sum(sums[1]) / order
 
     for x in range(6):
-        for copy in diagonal_copies(x) + partial_copies(x) + (corner_copies(x) if eta else []):
+        for copy in diagonal_copies(x):
+            copy.wait_send()
+    for n in range(7):
+        for copy in partial_copies(n) + (corner_copies(n) if eta else []):
             copy.wait_send()
     for turn in range(2):
         for stage in range(2):
@@ -423,15 +458,14 @@
                 return carry
 
             lax.fori_loop(1, (n_row, n_col)[stage], wait, 0)
-    first_out.wait()
-    second_out.wait()
 
 
 def call(eta, n_row, n_col, density, hamiltonian, offsets, branch):
     blocks = density.shape[2:]
     order = float(n_row * n_col * blocks[1] * blocks[2])
-    extra = 6 if eta else 1
+    extra = 7 if eta else 1
     any_space = pl.BlockSpec(memory_space=pl.ANY)
+    vmem = pl.BlockSpec(memory_space=pltpu.VMEM)
     smem = pl.BlockSpec(memory_space=pltpu.SMEM)
     dma = pltpu.SemaphoreType.DMA
     width = max(n_row, n_col)
@@ -443,7 +477,7 @@
             jax.ShapeDtypeStruct((2,), F32),
         ),
         in_specs=[smem, smem, any_space, any_space],
-        out_specs=(any_space, any_space, smem),
+        out_specs=(vmem, vmem, smem),
         scratch_shapes=[
             pltpu.VMEM((7, 2, B, B), F32),
             pltpu.VMEM((7, 2, B, B), F32),
@@ -452,25 +486,24 @@
             pltpu.VMEM((6, 6, 2, B, B), BF16),
             pltpu.VMEM((6, 6, 2, B, B), BF16),
             pltpu.VMEM((6, 6, 2, B, B), BF16),
-            pltpu.VMEM((6, 4, 2, B, B), F32),
-            pltpu.VMEM((6, 2, 2, B, B), F32),
-            pltpu.VMEM((6, 2, 2, B, B), F32),
-            pltpu.VMEM((6, 2, B, B), F32),
+            pltpu.VMEM((6, PACKED, B), F32),
+            pltpu.VMEM((6, 4, PACKED, B), F32),
+            pltpu.VMEM((2, 2, B, B), F32),
+            pltpu.VMEM((7, 2, PACKED, B), F32),
+            pltpu.VMEM((7, 2, PACKED, B), F32),
+            pltpu.VMEM((7, 2, B, B), F32),
             pltpu.VMEM((extra, 3, 2, 2, B, B), F32),
             [pltpu.VMEM((3, 2, 2, B, B), F32)] * extra,
             pltpu.VMEM((2, 2, 2, 8, B), F32),
             pltpu.VMEM((2, 2, width, 2, 8, B), F32),
-            pltpu.VMEM((7, 2, B, B), F32),
-            pltpu.VMEM((7, 2, B, B), F32),
             pltpu.SMEM((5, 8), I32),
-            dma((2,)),
             dma((2,)),
             dma((6, 4)),
             dma((6, 4)),
-            dma((6, 2)),
-            dma((6, 2)),
-            dma((6, 6)),
-            dma((6, 6)),
+            dma((7, 2)),
+            dma((7, 2)),
+            dma((7, 6)),
+            dma((7, 6)),
             dma((2, 2, width)),
             dma((2, 2, width)),
         ],
@@ -482,21 +515,12 @@
 
 
 def pattern_class(offsets):
-    rows, cols = offsets[:, 0], offsets[:, 1]
-    layers = offsets[:, 2] % 2
-
-    def find(a, b):
-        here = (rows == a) & (cols == b)
-        return jnp.any(here), jnp.sum(jnp.where(here, layers, 0))
-
-    has_a, layer_a = find(1, 0)
-    has_b, layer_b = find(0, 1)
-    has_c, layer_c = find(1, 1)
-    has_d, layer_d = find(1, -1)
-    pair = has_a & has_b
-    plus = pair & has_c & ((layer_a + layer_b + layer_c) % 2 == 0)
-    minus = pair & has_d & ((layer_a + layer_b + layer_d) % 2 == 0)
-    return jnp.where(plus, 1, jnp.where(minus, 2, 0)).astype(I32)
+    rows, cols, layers = offsets[:, 0], offsets[:, 1], offsets[:, 2] & 1
+    kind = jnp.where(rows == 1, jnp.where(cols == 0, 1, jnp.where(cols == 1, 64, 512)), 8)
+    leads = (rows == 1) | ((rows == 0) & (cols == 1))
+    code = jnp.sum(jnp.where(leads, kind + (layers << 12), 0))
+    seen, even = code & 4095, (code & 4096) == 0
+    return jnp.where(even & (seen == 73), 1, jnp.where(even & (seen == 521), 2, 0)).astype(I32)
 
 
 def solution(mesh):

time: 103 us -> 72.6 us (0.70)
  Pallas kernels: 87.8 us -> 64.8 us
  between operations: 5.85 us -> 1.97 us
  other arithmetic: 4.06 us -> 1.44 us
    pallas_call x1, Pallas kernels: 87.8 us -> 64.8 us  [call(): pl.pallas_call(functools.partial(kernel, eta, n_row, n_col, order), out_s...]
    reduce_or x4 -> x0, other arithmetic: 3.31 us -> none  [find(): return (jnp.any(here), jnp.sum(jnp.where(here, layers, 0)))]
where the time goes in v2:
time: 72.6 us; the launch traced here: 72.1 us
  Pallas kernels  64.8 us (89%)
  local copies, waits for them, and re-layouts  3.7 us (5%)
  between operations  1.97 us (3%)
  other arithmetic  1.44 us (2%)
    pallas_call x1, Pallas kernels, call(): pl.pallas_call(functools.partial(kernel, eta, n_row, n_col, order), out_s...  64.8 us
    unnamed x7, local copies, waits for them, and re-layouts  3.02 us

profile of v2, /device:TPU:32, one launch (start us, length us, event | category | flops | bytes accessed | tf_op | source)
XLA Modules:
  0.0 72.1 jit_solution(8078252860001483515)
XLA Ops:
  0.6 1.4 %fusion.1 = s32[]{:T(128)} fusion(s32[7,3]{0,1:T(4,128)} %param.9), kind=kLoop, calls=%fused_computation.5 | loop fusion | flops 97 | bytes 88 | tf_op jit(solution)/shard_map/reduce_sum | solution.py:521
  3.4 0.0 copy-start
  3.4 0.0 copy-start.1
  3.4 0.7 copy-done
  4.1 0.0 copy-done.1
  4.1 65.7 %conditional.1 = ((f32[1,1,7,2,128,128]{5,4,3,2,1,0:T(8,128)S(1)}, f32[1,1,7,2,128,128]{5,4,3,2,1,0:T(8,128)S(1)}, f32[2]{0:T(128)S(1)})) conditional(s32[]{:T(128)} %clamp.3, (s32[7,3]{0,1:T(4,128)S(1)}, s32[3]{0:T(128)S(1)}, f32[1,1,7,2,128,128]{5,4,3,2,1,0:T(8,128)}, f32[1,1,7,2,128,128]{5,4,3,2,1,0:T(8,128)}) %tuple.40, ...), branch_computations={%region_1.2_spmd, %region_2.3_spmd, %region_3.4_spmd} | conditional | bytes 176 | solution.py:531
  4.1 0.7 copy.16.off_ref
  4.7 64.8 %sp2_open.1 = (f32[1,1,7,2,128,128]{5,4,3,2,1,0:T(8,128)S(1)}, f32[1,1,7,2,128,128]{5,4,3,2,1,0:T(8,128)S(1)}, f32[2]{0:T(128)S(1)}) custom-call(s32[7,3]{1,0:T(8,128)} %copy.16.off_ref, s32[3]{0:T(128)S(1)} %get-tuple-element.25.branch_ref, f32[1,1,7,2,128,128]{5,4,3,2,1,0:T(8,128)} %get-tuple-element.26.x_hbm, ...), custom_call_target="tpu_custom_call" | custom-call | tf_op jit(solution)/shard_map/cond/branch_0_fun/sp2_open/pallas_call | solution.py:472
  69.8 0.9 %copy.31 = f32[1,1,7,2,128,128]{5,4,3,2,1,0:T(8,128)} copy(f32[1,1,7,2,128,128]{5,4,3,2,1,0:T(8,128)S(1)} %get-tuple-element.75) | data formatting | bytes 1835008
  70.7 0.9 %copy.32 = f32[1,1,7,2,128,128]{5,4,3,2,1,0:T(8,128)} copy(f32[1,1,7,2,128,128]{5,4,3,2,1,0:T(8,128)S(1)} %get-tuple-element.76) | data formatting | bytes 1835008
  71.6 0.5 copy.33
Async XLA Ops:
  3.4 0.7 copy-start
  3.4 0.7 copy-start.1

commit v3 on v2

--- a/solution.py
+++ b/solution.py
@@ -59,7 +59,7 @@
     eta, n_row, n_col, order,
     off_ref, branch_ref, x_hbm, h_hbm,
     new_ref, grad_ref, tot_ref,
-    raw_x, raw_h, cf, eh, el, dh, dl, sd, rd, parts, sp, rp, ow, ox, rx, ar_src, ar, tab,
+    raw_x, raw_h, cf, eh, el, dh, dl, sd, rd, parts, sp, rp, ow, ox, st, sa, ra, ah, al, ext, rv, rt, ar_src, ar, tab,
     in_sem, d_send, d_recv, p_send, p_recv, x_send, x_recv, ar_send, ar_recv,
 ):
     p, q = lax.axis_index(ROW), lax.axis_index(COL)
@@ -99,13 +99,7 @@
     lax.fori_loop(1, n_row, greet_row, 0)
     lax.fori_loop(1, n_col, greet_col, 0)
     greeted = n_row + n_col - 2
-    if eta:
-        corners = [(up, left if eta > 0 else right), (down, right if eta > 0 else left)]
-        for corner in corners:
-            pl.semaphore_signal(barrier, inc=1, device_id=corner, device_id_type=MESH_ID)
-        greeted += 2
-
-    off = [[off_ref[t, c] for c in range(3)] for t in range(7)]
+    off = [[off_ref[c, t] for c in range(3)] for t in range(7)]
     lay = [lax.rem(o[2] + 2, 2) for o in off]
     zero = [(o[0] == 0) & (o[1] == 0) & (s == 0) for o, s in zip(off, lay)]
     slots = [total(zero, range(7))]
@@ -199,24 +193,114 @@
             for g in range(2)
         ]
 
-    def corner_copies(n):
-        copies = []
-        for j in range(3):
-            for g in range(2):
-                row_to = (up, down)[g]
-                col_to = (left, right)[g] if eta > 0 else (right, left)[g]
-                target = ((row_to, q), (p, col_to), (row_to, col_to))[j]
-                copies.append(
-                    pltpu.make_async_remote_copy(
-                        src_ref=ox.at[n, j, g],
-                        dst_ref=rx[n].at[j, 1 - g],
-                        send_sem=x_send.at[n, 2 * j + g],
-                        recv_sem=x_recv.at[n, 2 * j + g],
-                        device_id=target,
-                        device_id_type=MESH_ID,
-                    )
-                )
-        return copies
+    toward = ((left, right) if eta > 0 else (right, left)) if eta else None
+
+    def corner_copy(src, dst, x, i, target):
+        return pltpu.make_async_remote_copy(
+            src_ref=src,
+            dst_ref=dst,
+            send_sem=x_send.at[x, i],
+            recv_sem=x_recv.at[x, i],
+            device_id=target,
+            device_id_type=MESH_ID,
+        )
+
+    def operand_copies(x):
+        targets = ((p, toward[0]), (p, toward[1]), (up, q), (down, q))
+        return [corner_copy(sa.at[x, i], ra.at[x, i], x, i, target) for i, target in enumerate(targets)]
+
+    def first_copies(n):
+        return [corner_copy(ox.at[n, 0, g], rv[n].at[1 - g], n, 4 + g, ((up, q), (down, q))[g]) for g in range(2)]
+
+    def second_copies(n):
+        return [corner_copy(st.at[n, g], rt[n].at[1 - g], n, 6 + g, ((up, q), (down, q))[g]) for g in range(2)]
+
+    def corner_all(n):
+        return operand_copies(n) + first_copies(n) + second_copies(n) if eta else []
+
+    def send_operands(x):
+        if not eta:
+            return
+        for i, copy in enumerate(operand_copies(x)):
+            sa[x, i] = cf[x, (1, 2, 5, 6)[i]]
+            copy.start()
+
+    def receive_operands(x, same=None):
+        if not eta:
+            return
+        for copy in operand_copies(x):
+            copy.wait_recv()
+
+        def body(i, carry):
+            for s in range(2):
+                value = ra[x, i, s]
+                if same is not None:
+                    value = value + same * (ah[X2, i, s].astype(F32) + al[X2, i, s].astype(F32))
+                ah[x, i, s], al[x, i, s] = split(value)
+            return carry
+
+        lax.fori_loop(0, 4, body, 0)
+
+    def summed(terms):
+        return functools.reduce(jnp.add, terms)
+
+    def send_corners(n, x, g=None):
+        if not eta:
+            return
+        pairs = [(x, x)] if g is None else [(g, x), (x, g)]
+
+        def body(i, carry):
+            sign, s = i // 2, lax.rem(i, 2)
+            other = lax.rem(s + steps[3][2], 2)
+            ka, kb, kc = 1 + sign, 3 + sign, 5 + sign
+            ox[n, 0, sign, s] = summed([dot_tn(edge(u, kb, s), edge(v, kc, s)) for u, v in pairs])
+            ox[n, 1, sign, s] = summed([dot_nt(edge(u, kc, s), edge(v, ka, other)) for u, v in pairs])
+            ox[n, 2, sign, s] = summed([dot_nn([edge(u, kb, s)], [edge(v, ka, other)]) for u, v in pairs])
+            return carry
+
+        lax.fori_loop(0, 4, body, 0)
+        for copy in first_copies(n):
+            copy.start()
+
+    def send_seconds(n, x, g=None):
+        if not eta:
+            return
+        pairs = [(x, x)] if g is None else [(g, x), (x, g)]
+
+        def operand(m, i, s):
+            return ah[m, i, s], al[m, i, s]
+
+        def body(i, carry):
+            sign, s = i // 2, lax.rem(i, 2)
+            st[n, sign, s] = summed([dot_tn(edge(u, 4 - sign, s), operand(v, sign, s)) for u, v in pairs])
+            return carry
+
+        lax.fori_loop(0, 4, body, 0)
+        for copy in second_copies(n):
+            copy.start()
+
+        def rest(i, carry):
+            sign, s = i // 2, lax.rem(i, 2)
+            other = lax.rem(s + steps[1][2], 2)
+            ext[3 - sign, s] = ox[n, 1, 1 - sign, s] + summed(
+                [dot_nn([operand(u, sign, s)], [operand(v, 3 - sign, other)]) for u, v in pairs]
+            )
+            return carry
+
+        lax.fori_loop(0, 4, rest, 0)
+
+    def gather_corners(n):
+        for copy in first_copies(n) + second_copies(n):
+            copy.wait_recv()
+        la, lb, lc = steps[1][2], steps[3][2], steps[5][2]
+
+        def body(i, carry):
+            sign, s = i // 2, lax.rem(i, 2)
+            ext[sign, s] = ox[n, 0, sign, lax.rem(s + lb, 2)] + rv[n][sign, lax.rem(s + lc, 2)].T
+            ext[4 + sign, s] = ox[n, 2, sign, s] + rt[n][sign, lax.rem(s + la, 2)].T
+            return carry
+
+        lax.fori_loop(0, 4, body, 0)
 
     def edge(x, k, s):
         return eh[x, k - 1, s], el[x, k - 1, s]
@@ -253,36 +337,11 @@
         for sign, copy in enumerate(partial_copies(n)):
             pack(sp.at[n, sign], parts[sign, 0], parts[sign, 1])
             copy.start()
-        if not eta:
-            return
-
-        def corners_body(i, carry):
-            sign, s = i // 2, lax.rem(i, 2)
-            other = lax.rem(s + steps[3][2], 2)
-            pairs = [(x, x)] if g is None else [(g, x), (x, g)]
-            ka, kb, kc = 1 + sign, 3 + sign, 5 + sign
-            ox[n, 0, sign, s] = functools.reduce(
-                jnp.add, [dot_tn(edge(u, kb, s), edge(v, kc, s)) for u, v in pairs]
-            )
-            ox[n, 1, sign, s] = functools.reduce(
-                jnp.add, [dot_nt(edge(u, kc, s), edge(v, ka, other)) for u, v in pairs]
-            )
-            ox[n, 2, sign, s] = functools.reduce(
-                jnp.add, [dot_nn([edge(u, kb, s)], [edge(v, ka, other)]) for u, v in pairs]
-            )
-            return carry
-
-        lax.fori_loop(0, 4, corners_body, 0)
-        for copy in corner_copies(n):
-            copy.start()
-
-    def update_edges(n, sign, x, out, g=None, extra=None):
+
+    def update_edges(n, sign, x, out, g=None):
         base = x if g is None else g
         if eta:
-            for copy in corner_copies(n) + (corner_copies(6) if extra is not None else []):
-                copy.wait_recv()
-        lb = steps[3][2]
-        lc = steps[5][2]
+            gather_corners(n)
 
         def body(i, carry):
             k = i + 1
@@ -302,14 +361,7 @@
                     g_edge = (eh[g, i, s], el[g, i, s])
                     product = dot_nn([g_left, x_left, g_edge, x_edge], [x_edge, g_edge, x_right, g_right])
                 if eta:
-                    j, sg = i // 2, lax.rem(i, 2)
-                    mine = jnp.where(j == 0, lb, 0)
-                    theirs = jnp.where(j == 1, lb, lc)
-                    corner = ox[n, j, sg, lax.rem(s + mine, 2)] + rx[n][j, sg, lax.rem(s + theirs, 2)].T
-                    product = product + corner
-                    if extra is not None:
-                        corner = ox[6, j, sg, lax.rem(s + mine, 2)] + rx[6][j, sg, lax.rem(s + theirs, 2)].T
-                        product = product + extra * corner
+                    product = product + ext[i, s]
                 value = (1.0 + sign) * cf[base, k, s] - sign * product
                 cf[out, k, s] = value
                 if out < X3:
@@ -367,6 +419,9 @@
     def tiles(value):
         return jnp.sum(value.reshape(-1, 8, B), axis=0)
 
+    def lanes(first, second):
+        return cat([jnp.sum(v, axis=0, keepdims=True) for v in (first, second)], 0)
+
     def trace_of(x):
         return functools.reduce(jnp.add, [tiles(jnp.where(eye, cf[x, 0, s], 0.0)) for s in range(2)])
 
@@ -387,33 +442,48 @@
     take_in(0, X0)
     pl.semaphore_wait(barrier, greeted)
     send_diagonal(X0)
+    send_operands(X0)
     split_edges(X0)
     split_diagonal(X0)
     send_partials(0, X0)
+    send_corners(0, X0)
     take_in(1, HAM)
     split_edges(HAM)
     split_diagonal(HAM)
     update_diagonal(0, signs[0], X0, X1)
+    receive_operands(X0)
+    send_seconds(0, X0)
     receive_diagonal(X0)
     update_edges(0, signs[0], X0, X1)
+    send_operands(X1)
     send_partials(1, X1)
+    send_corners(1, X1)
     send_diagonal(HAM)
+    send_operands(HAM)
     update_diagonal(1, signs[1], X1, X2)
+    receive_operands(X1)
+    send_seconds(1, X1)
     receive_diagonal(X1)
     update_edges(1, signs[1], X1, X2)
+    send_operands(X2)
     last = signs[2]
     send_partials(3, X2, HAM)
     occupied = (1.0 + last) * trace_of(X2) - last * dot_all(X2, X2)
-    reduce_start(0, 0, jnp.stack([occupied, occupied]))
+    reduce_start(0, 0, lanes(occupied, occupied))
+    send_corners(3, X2, HAM)
     send_partials(6, X1, X2)
     reduce_start(0, 1, reduce_end(0, 0))
     update_diagonal(3, last, X2, G2, HAM)
+    receive_operands(HAM)
+    receive_operands(X2)
+    send_seconds(3, X2, HAM)
     receive_diagonal(HAM)
     receive_diagonal(X2)
     update_edges(3, last, X2, G2, HAM)
+    send_operands(G2)
     send_partials(4, X1, G2)
     send_partials(2, X2)
-    excess = jnp.sum(reduce_end(0, 1)[0]) / order - 0.5
+    excess = jnp.sum(reduce_end(0, 1)[0:1]) / order - 0.5
     one, same = (1.0 + last) * excess, -2.0 * last * excess
 
     def complete(k, carry):
@@ -428,27 +498,36 @@
         cf[G2, 0, s] = cf[G2, 0, s] + jnp.where(eye, one, 0.0) + same * cf[X2, 0, s]
     split_diagonal(G2)
     update_diagonal(4, signs[1], X1, G1, G2, (one, same))
+    send_corners(4, X1, G2)
+    receive_operands(G2, same)
+    send_seconds(4, X1, G2)
     receive_diagonal(G2, lambda value: jnp.where(eye, one, 0.0) + same * value)
-    update_edges(4, signs[1], X1, G1, G2, same)
+    update_edges(4, signs[1], X1, G1, G2)
+    send_operands(G1)
     send_partials(5, X0, G1)
+    send_corners(5, X0, G1)
+    send_corners(2, X2)
+    send_seconds(2, X2)
     update_edges(2, last, X2, X3)
     update_diagonal(2, last, X2, X3)
-    reduce_start(1, 0, jnp.stack([dot_all(HAM, X3), trace_of(X3)]))
+    reduce_start(1, 0, lanes(dot_all(HAM, X3), trace_of(X3)))
     update_diagonal(5, signs[0], X0, G0, G1)
     put_out(X3, new_ref)
     reduce_start(1, 1, reduce_end(1, 0))
+    receive_operands(G1)
+    send_seconds(5, X0, G1)
     receive_diagonal(G1)
     update_edges(5, signs[0], X0, G0, G1)
     put_out(G0, grad_ref)
     sums = reduce_end(1, 1)
-    tot_ref[0] = jnp.sum(sums[0]) / order
-    tot_ref[1] = jnp.sum(sums[1]) / order
+    tot_ref[0] = jnp.sum(sums[0:1]) / order
+    tot_ref[1] = jnp.sum(sums[1:2]) / order
 
     for x in range(6):
         for copy in diagonal_copies(x):
             copy.wait_send()
     for n in range(7):
-        for copy in partial_copies(n) + (corner_copies(n) if eta else []):
+        for copy in partial_copies(n) + (corner_all(n) if n < 6 else []):
             copy.wait_send()
     for turn in range(2):
         for stage in range(2):
@@ -463,7 +542,7 @@
 def call(eta, n_row, n_col, density, hamiltonian, offsets, branch):
     blocks = density.shape[2:]
     order = float(n_row * n_col * blocks[1] * blocks[2])
-    extra = 7 if eta else 1
+    extra = 6 if eta else 1
     any_space = pl.BlockSpec(memory_space=pl.ANY)
     vmem = pl.BlockSpec(memory_space=pltpu.VMEM)
     smem = pl.BlockSpec(memory_space=pltpu.SMEM)
@@ -493,17 +572,24 @@
             pltpu.VMEM((7, 2, PACKED, B), F32),
             pltpu.VMEM((7, 2, B, B), F32),
             pltpu.VMEM((extra, 3, 2, 2, B, B), F32),
-            [pltpu.VMEM((3, 2, 2, B, B), F32)] * extra,
-            pltpu.VMEM((2, 2, 2, 8, B), F32),
-            pltpu.VMEM((2, 2, width, 2, 8, B), F32),
+            pltpu.VMEM((extra, 2, 2, B, B), F32),
+            pltpu.VMEM((extra, 4, 2, B, B), F32),
+            pltpu.VMEM((extra, 4, 2, B, B), F32),
+            pltpu.VMEM((extra, 4, 2, B, B), BF16),
+            pltpu.VMEM((extra, 4, 2, B, B), BF16),
+            pltpu.VMEM((6, 2, B, B), F32),
+            [pltpu.VMEM((2, 2, B, B), F32)] * extra,
+            [pltpu.VMEM((2, 2, B, B), F32)] * extra,
+            pltpu.VMEM((2, 2, 2, B), F32),
+            pltpu.VMEM((2, 2, width, 2, B), F32),
             pltpu.SMEM((5, 8), I32),
             dma((2,)),
             dma((6, 4)),
             dma((6, 4)),
             dma((7, 2)),
             dma((7, 2)),
-            dma((7, 6)),
-            dma((7, 6)),
+            dma((6, 8)),
+            dma((6, 8)),
             dma((2, 2, width)),
             dma((2, 2, width)),
         ],
@@ -511,7 +597,7 @@
             collective_id=1 + eta, has_side_effects=True, vmem_limit_bytes=56 * 1024 * 1024
         ),
         name="sp2_" + ("mirrored", "open", "closed")[1 + eta],
-    )(offsets, branch, density, hamiltonian)
+    )(offsets.T, branch, density, hamiltonian)
 
 
 def pattern_class(offsets):

time: 72.6 us -> 68.1 us (0.938)
  Pallas kernels: 64.8 us -> 60.3 us
    pallas_call x1, Pallas kernels: 64.8 us -> 60.3 us  [call(): pl.pallas_call(functools.partial(kernel, eta, n_row, n_col, order), out_s...]
where the time goes in v3:
time: 68.1 us; the launch traced here: 67 us
  Pallas kernels  60.3 us (89%)
  local copies, waits for them, and re-layouts  3.02 us (4%)
  between operations  1.97 us (3%)
  other arithmetic  1.44 us (2%)
    pallas_call x1, Pallas kernels, call(): pl.pallas_call(functools.partial(kernel, eta, n_row, n_col, order), out_s...  60.3 us
    unnamed x7, local copies, waits for them, and re-layouts  3.02 us
    reduce_sum x1, other arithmetic, pattern_class(): code = jnp.sum(jnp.where(leads, kind + (layers << 12), 0))  1.44 us

profile of v3, /device:TPU:32, one launch (start us, length us, event | category | flops | bytes accessed | tf_op | source)
XLA Modules:
  0.0 67.0 jit_solution(12261226886781537270)
XLA Ops:
  0.6 1.4 %fusion.1 = s32[]{:T(128)} fusion(s32[7,3]{0,1:T(4,128)} %param.9), kind=kLoop, calls=%fused_computation.5 | loop fusion | flops 97 | bytes 88 | tf_op jit(solution)/shard_map/reduce_sum | solution.py:607
  3.4 0.0 copy-start
  3.4 0.0 copy-start.1
  3.4 0.7 copy-done
  4.1 0.0 copy-done.1
  4.1 60.5 %conditional.1 = ((f32[1,1,7,2,128,128]{5,4,3,2,1,0:T(8,128)S(1)}, f32[1,1,7,2,128,128]{5,4,3,2,1,0:T(8,128)S(1)}, f32[2]{0:T(128)S(1)})) conditional(s32[]{:T(128)} %clamp.3, (s32[7,3]{0,1:T(4,128)S(1)}, s32[3]{0:T(128)S(1)}, f32[1,1,7,2,128,128]{5,4,3,2,1,0:T(8,128)}, f32[1,1,7,2,128,128]{5,4,3,2,1,0:T(8,128)}) %tuple.37, ...), branch_computations={%region_1.2_spmd, %region_2.3_spmd, %region_3.4_spmd} | conditional | bytes 8 | solution.py:617
  4.1 60.3 %sp2_open.1 = (f32[1,1,7,2,128,128]{5,4,3,2,1,0:T(8,128)S(1)}, f32[1,1,7,2,128,128]{5,4,3,2,1,0:T(8,128)S(1)}, f32[2]{0:T(128)S(1)}) custom-call(s32[3,7]{1,0:T(4,128)S(1)} %bitcast.3, s32[3]{0:T(128)S(1)} %get-tuple-element.25.branch_ref, f32[1,1,7,2,128,128]{5,4,3,2,1,0:T(8,128)} %get-tuple-element.26.x_hbm, f32[1,1,7,2,128,128]{5,4,3,2,1,0:T(8,128)} %get-tuple-element.27.h_hbm), custom_call_target="tpu_custom_call" | custom-call | tf_op jit(solution)/shard_map/cond/branch_0_fun/sp2_open/pallas_call | solution.py:551
  64.6 0.9 %copy.28 = f32[1,1,7,2,128,128]{5,4,3,2,1,0:T(8,128)} copy(f32[1,1,7,2,128,128]{5,4,3,2,1,0:T(8,128)S(1)} %get-tuple-element.63) | data formatting | bytes 1835008
  65.5 0.9 %copy.29 = f32[1,1,7,2,128,128]{5,4,3,2,1,0:T(8,128)} copy(f32[1,1,7,2,128,128]{5,4,3,2,1,0:T(8,128)S(1)} %get-tuple-element.64) | data formatting | bytes 1835008
  66.4 0.5 copy.30
Async XLA Ops:
  3.4 0.7 %copy-start = (s32[7,3]{0,1:T(4,128)S(1)}, s32[7,3]{0,1:T(4,128)}, u32[]{:S(2)}) copy-start(s32[7,3]{0,1:T(4,128)} %param.9) | copy-start | bytes 256
  3.4 0.7 %copy-start.1 = (s32[3]{0:T(128)S(1)}, s32[3]{0:T(128)}, u32[]{:S(2)}) copy-start(s32[3]{0:T(128)} %param.10) | copy-start | bytes 40

commit v4 on v3

--- a/solution.py
+++ b/solution.py
@@ -127,8 +127,9 @@
     signs = [(2 * branch_ref[k] - 1).astype(F32) for k in range(3)]
     keep = [jnp.where(steps[1 + 2 * j][0] != 0, 1.0, 0.0).astype(F32) for j in range(3)]
 
-    def take_in(which, x):
-        loads[which].wait()
+    def take_in(which, x, first, last):
+        if not first:
+            loads[which].wait()
         raw = (raw_x, raw_h)[which]
 
         def body(k, carry):
@@ -136,7 +137,7 @@
             cf[x, k] = raw[slot]
             return carry
 
-        lax.fori_loop(0, 7, body, 0)
+        lax.fori_loop(first, last, body, 0)
 
     def split_edges(x):
         def body(i, carry):
@@ -152,19 +153,18 @@
             for place in (1, 4):
                 dh[x, place, s], dl[x, place, s] = high, low
 
+    def diagonal_copy(x, i):
+        return pltpu.make_async_remote_copy(
+            src_ref=sd.at[x],
+            dst_ref=rd.at[x, i],
+            send_sem=d_send.at[x, i],
+            recv_sem=d_recv.at[x, i],
+            device_id=((p, right), (p, left), (up, q), (down, q))[i],
+            device_id_type=MESH_ID,
+        )
+
     def diagonal_copies(x):
-        targets = ((p, right), (p, left), (up, q), (down, q))
-        return [
-            pltpu.make_async_remote_copy(
-                src_ref=sd.at[x],
-                dst_ref=rd.at[x, i],
-                send_sem=d_send.at[x, i],
-                recv_sem=d_recv.at[x, i],
-                device_id=target,
-                device_id_type=MESH_ID,
-            )
-            for i, target in enumerate(targets)
-        ]
+        return [diagonal_copy(x, i) for i in range(4)]
 
     def send_diagonal(x):
         pack(sd.at[x], cf[x, 0, 0], cf[x, 0, 1])
@@ -172,8 +172,8 @@
             copy.start()
 
     def receive_diagonal(x, extra=None):
-        for i, copy in enumerate(diagonal_copies(x)):
-            copy.wait_recv()
+        for i in (2, 3, 0, 1):
+            diagonal_copy(x, i).wait_recv()
             place = (0, 2, 3, 5)[i]
             for s, value in enumerate(unpack(rd[x, i, 0:B, :], rd[x, i, B : B + 1, :])):
                 if extra is not None:
@@ -416,6 +416,13 @@
         lax.fori_loop(1, count, wait, 0)
         return lax.fori_loop(1, count, lambda d, v: v + ar[turn, stage, d], ar_src[turn, stage])
 
+    def sent(turn, stage):
+        def wait(d, carry):
+            reduce_copy(turn, stage, d).wait_send()
+            return carry
+
+        lax.fori_loop(1, (n_row, n_col)[stage], wait, 0)
+
     def tiles(value):
         return jnp.sum(value.reshape(-1, 8, B), axis=0)
 
@@ -439,15 +446,16 @@
 
         lax.fori_loop(0, 7, body, 0)
 
-    take_in(0, X0)
+    take_in(0, X0, 0, 1)
     pl.semaphore_wait(barrier, greeted)
     send_diagonal(X0)
+    take_in(0, X0, 1, 7)
     send_operands(X0)
     split_edges(X0)
     split_diagonal(X0)
     send_partials(0, X0)
     send_corners(0, X0)
-    take_in(1, HAM)
+    take_in(1, HAM, 0, 7)
     split_edges(HAM)
     split_diagonal(HAM)
     update_diagonal(0, signs[0], X0, X1)
@@ -472,8 +480,8 @@
     reduce_start(0, 0, lanes(occupied, occupied))
     send_corners(3, X2, HAM)
     send_partials(6, X1, X2)
+    update_diagonal(3, last, X2, G2, HAM)
     reduce_start(0, 1, reduce_end(0, 0))
-    update_diagonal(3, last, X2, G2, HAM)
     receive_operands(HAM)
     receive_operands(X2)
     send_seconds(3, X2, HAM)
@@ -483,7 +491,10 @@
     send_operands(G2)
     send_partials(4, X1, G2)
     send_partials(2, X2)
-    excess = jnp.sum(reduce_end(0, 1)[0:1]) / order - 0.5
+    energy = 0.5 * ((1.0 + last) * dot_all(HAM, X2) + dot_all(X2, G2))
+    reduce_start(1, 0, lanes(energy, energy))
+    occupation = jnp.sum(reduce_end(0, 1)[0:1]) / order
+    excess = occupation - 0.5
     one, same = (1.0 + last) * excess, -2.0 * last * excess
 
     def complete(k, carry):
@@ -506,37 +517,33 @@
     send_operands(G1)
     send_partials(5, X0, G1)
     send_corners(5, X0, G1)
+    reduce_start(1, 1, reduce_end(1, 0))
     send_corners(2, X2)
     send_seconds(2, X2)
     update_edges(2, last, X2, X3)
     update_diagonal(2, last, X2, X3)
-    reduce_start(1, 0, lanes(dot_all(HAM, X3), trace_of(X3)))
+    put_out(X3, new_ref)
     update_diagonal(5, signs[0], X0, G0, G1)
-    put_out(X3, new_ref)
-    reduce_start(1, 1, reduce_end(1, 0))
     receive_operands(G1)
     send_seconds(5, X0, G1)
+    for x in range(5):
+        for copy in diagonal_copies(x):
+            copy.wait_send()
+    for n in range(7):
+        for copy in partial_copies(n) + (corner_all(n) if n < 6 else []):
+            copy.wait_send()
+    for turn, stage in ((0, 0), (0, 1), (1, 0)):
+        sent(turn, stage)
     receive_diagonal(G1)
     update_edges(5, signs[0], X0, G0, G1)
     put_out(G0, grad_ref)
     sums = reduce_end(1, 1)
     tot_ref[0] = jnp.sum(sums[0:1]) / order
-    tot_ref[1] = jnp.sum(sums[1:2]) / order
-
-    for x in range(6):
-        for copy in diagonal_copies(x):
-            copy.wait_send()
-    for n in range(7):
-        for copy in partial_copies(n) + (corner_all(n) if n < 6 else []):
-            copy.wait_send()
-    for turn in range(2):
-        for stage in range(2):
-
-            def wait(d, carry):
-                reduce_copy(turn, stage, d).wait_send()
-                return carry
-
-            lax.fori_loop(1, (n_row, n_col)[stage], wait, 0)
+    tot_ref[1] = occupation
+
+    for copy in diagonal_copies(G1):
+        copy.wait_send()
+    sent(1, 1)
 
 
 def call(eta, n_row, n_col, density, hamiltonian, offsets, branch):

time: 68.1 us -> 64.6 us (0.949); the launches traced: 67 us -> 64.4 us
  Pallas kernels: 60.3 us -> 57.8 us
    pallas_call x1, Pallas kernels: 60.3 us -> 57.8 us  [call(): pl.pallas_call(functools.partial(kernel, eta, n_row, n_col, order), out_s...]
where the time goes in v4:
time: 64.6 us; the launch traced here: 64.4 us
  Pallas kernels  57.8 us (89%)
  local copies, waits for them, and re-layouts  3.02 us (5%)
  between operations  1.97 us (3%)
  other arithmetic  1.44 us (2%)
    pallas_call x1, Pallas kernels, call(): pl.pallas_call(functools.partial(kernel, eta, n_row, n_col, order), out_s...  57.8 us
    unnamed x7, local copies, waits for them, and re-layouts  3.02 us
    reduce_sum x1, other arithmetic, pattern_class(): code = jnp.sum(jnp.where(leads, kind + (layers << 12), 0))  1.44 us

profile of v4, /device:TPU:32, one launch (start us, length us, event | category | flops | bytes accessed | tf_op | source)
XLA Modules:
  0.0 64.4 jit_solution(12107585793685432700)
XLA Ops:
  0.6 1.4 %fusion.1 = s32[]{:T(128)} fusion(s32[7,3]{0,1:T(4,128)} %param.9), kind=kLoop, calls=%fused_computation.5 | loop fusion | flops 97 | bytes 88 | tf_op jit(solution)/shard_map/reduce_sum | solution.py:614
  3.4 0.0 copy-start
  3.4 0.0 copy-start.1
  3.4 0.7 %copy-done = s32[7,3]{0,1:T(4,128)S(1)} copy-done((s32[7,3]{0,1:T(4,128)S(1)}, s32[7,3]{0,1:T(4,128)}, u32[]{:S(2)}) %copy-start) | copy-done | bytes 108
  4.1 0.0 copy-done.1
  4.1 58.0 %conditional.1 = ((f32[1,1,7,2,128,128]{5,4,3,2,1,0:T(8,128)S(1)}, f32[1,1,7,2,128,128]{5,4,3,2,1,0:T(8,128)S(1)}, f32[2]{0:T(128)S(1)})) conditional(s32[]{:T(128)} %clamp.3, (s32[7,3]{0,1:T(4,128)S(1)}, s32[3]{0:T(128)S(1)}, f32[1,1,7,2,128,128]{5,4,3,2,1,0:T(8,128)}, f32[1,1,7,2,128,128]{5,4,3,2,1,0:T(8,128)}) %tuple.37, ...), branch_computations={%region_1.2_spmd, %region_2.3_spmd, %region_3.4_spmd} | conditional | bytes 8 | solution.py:624
  4.1 57.8 %sp2_open.1 = (f32[1,1,7,2,128,128]{5,4,3,2,1,0:T(8,128)S(1)}, f32[1,1,7,2,128,128]{5,4,3,2,1,0:T(8,128)S(1)}, f32[2]{0:T(128)S(1)}) custom-call(s32[3,7]{1,0:T(4,128)S(1)} %bitcast.3, s32[3]{0:T(128)S(1)} %get-tuple-element.25.branch_ref, f32[1,1,7,2,128,128]{5,4,3,2,1,0:T(8,128)} %get-tuple-element.26.x_hbm, f32[1,1,7,2,128,128]{5,4,3,2,1,0:T(8,128)} %get-tuple-element.27.h_hbm), custom_call_target="tpu_custom_call" | custom-call | tf_op jit(solution)/shard_map/cond/branch_0_fun/sp2_open/pallas_call | solution.py:558
  62.1 0.9 %copy.28 = f32[1,1,7,2,128,128]{5,4,3,2,1,0:T(8,128)} copy(f32[1,1,7,2,128,128]{5,4,3,2,1,0:T(8,128)S(1)} %get-tuple-element.63) | data formatting | bytes 1835008
  63.0 0.9 %copy.29 = f32[1,1,7,2,128,128]{5,4,3,2,1,0:T(8,128)} copy(f32[1,1,7,2,128,128]{5,4,3,2,1,0:T(8,128)S(1)} %get-tuple-element.64) | data formatting | bytes 1835008
  63.9 0.5 copy.30
Async XLA Ops:
  3.4 0.7 %copy-start = (s32[7,3]{0,1:T(4,128)S(1)}, s32[7,3]{0,1:T(4,128)}, u32[]{:S(2)}) copy-start(s32[7,3]{0,1:T(4,128)} %param.9) | copy-start | bytes 256
  3.4 0.7 %copy-start.1 = (s32[3]{0:T(128)S(1)}, s32[3]{0:T(128)}, u32[]{:S(2)}) copy-start(s32[3]{0:T(128)} %param.10) | copy-start | bytes 40
